TPU v7x, 128 devices: a whole 4x4x4 slice. The times are simulated.
128 devices in a mesh: ctx: 16 (over y, z), head: 8 (over x, core).
Axes of the slice: x: 4, y: 4, z: 4, core: 2. Of those that a mesh axis runs over, the one named last changes fastest.
Arguments:
- prompt_states: bfloat16 [8192, 2048], P('ctx')
- decode_states: bfloat16 [4, 2048], replicated
- lengths: int32 [4], replicated, may hold values from 1 to 4096, 8192 in all
- page_table: int32 [64], replicated, may hold values from 0 to 63, as said below
- w_query: bfloat16 [2048, 3072], P(None, 'head'), may hold values from -0.125 to 0.125
- w_down: bfloat16 [2048, 576], replicated, may hold values from -0.125 to 0.125
- kv_gain: float32 [512], replicated, may hold values from 0.1 to 1.9
- w_up: bfloat16 [512, 4096], P(None, 'head'), may hold values from -0.25 to 0.25
- w_out: bfloat16 [2048, 2048], P('head'), may hold values from -0.125 to 0.125
Outputs:
- prefill_out: bfloat16 [8192, 2048], P(('ctx', 'head'))
- paged_cache: bfloat16 [8192, 576], P('ctx')
- decode_out: bfloat16 [4, 2048], replicated
Inputs may be any that keep to these rules, and one draw needn't show every extreme that they name: page_table is a permutation of the 64 pages; the logical pages of ctx index c are c * 4 to c * 4 + 3, and physical page p lies on ctx index p // 4; logical page c * 4 + w has physical page ((c + s_w) mod 16) * 4 + w, where the shifts s_0 to s_(3) are distinct numbers of 0 to 16 - 1, the same for every c.
All inputs are finite; a program needn't handle non-finite values.
Results may differ from a plain program's by a relative error of at most 0.025.
Values may be sent and summed in bfloat16 or wider, within the bound.
No kernel may reach another device: no remote copies, remote signals or barrier semaphores. Data moves between devices by JAX's collectives and lax.ppermute only.
A program may use at most 192 MiB of HBM per device.

v0:
```python
import jax
import jax.numpy as jnp
from jax import lax
from jax.sharding import PartitionSpec as P

NOPE = 128
ROPE = 64
VDIM = 128
RANK = 512
PAGE = 128


ROPE_BASE = 50000.0
FAR_LOW = -1e30


def from_behind(block, axis, distance):
    devices = range(lax.axis_size(axis))
    route = [((i - distance) % len(devices), i) for i in devices]
    return lax.ppermute(block, axis, route)


def combined_all(value, axis, join):
    pieces = jax.tree.map(lambda part: lax.all_gather(part, axis), value)
    head = jax.tree.map(lambda part: part[0], pieces)
    tail = jax.tree.map(lambda part: part[1:], pieces)
    subtotal, _ = lax.scan(lambda subtotal, piece: (join(subtotal, piece), None), head, tail)
    return subtotal


def rope(vector, place):
    half = vector.shape[-1] // 2
    freq = ROPE_BASE ** (-(jnp.arange(half, dtype=jnp.float32) * 2.0 / vector.shape[-1]))
    angle = place[..., None] * freq
    first, second = (vector[..., :half], vector[..., half:])
    return jnp.concatenate(
        [
            first * jnp.cos(angle) - second * jnp.sin(angle),
            first * jnp.sin(angle) + second * jnp.cos(angle),
        ],
        -1,
    )


def token_info(index, lengths):
    ends = jnp.cumsum(lengths)
    starts = ends - lengths
    tenant = jnp.sum((index[:, None] >= ends[None, :]).astype(jnp.int32), 1)
    picked = jnp.sum(
        jnp.where(
            tenant[:, None] == jnp.arange(lengths.shape[0], dtype=jnp.int32)[None, :],
            starts[None, :],
            0,
        ),
        1,
    )
    return (tenant, index - picked)


def latent_of(states, w_down, kv_gain, place):
    lat = jnp.dot(states, w_down, preferred_element_type=jnp.float32)
    comp = lat[:, :RANK]
    comp = comp * lax.rsqrt(jnp.mean(comp * comp, -1, keepdims=True) + 1e-06) * kv_gain
    return jnp.concatenate([comp, rope(lat[:, RANK:], place)], 1).astype(jnp.bfloat16)


def queries(states, w_query, w_up, place):
    rows = states.shape[0]
    heads = w_query.shape[1] // (NOPE + ROPE)
    qfull = (
        jnp.dot(states, w_query, preferred_element_type=jnp.float32)
        .astype(jnp.bfloat16)
        .reshape(rows, heads, NOPE + ROPE)
    )
    w_key = w_up.reshape(RANK, heads, NOPE + VDIM)[:, :, :NOPE]
    qnope = jnp.einsum("thn,rhn->thr", qfull[..., :NOPE], w_key, preferred_element_type=jnp.float32)
    qrope = rope(qfull[..., NOPE:].astype(jnp.float32), place[:, None])
    scale = (NOPE + ROPE) ** (-0.5)
    return (jnp.concatenate([qnope, qrope], -1) * scale).astype(jnp.bfloat16)


def values_of(mixed, w_up):
    heads = w_up.shape[1] // (NOPE + VDIM)
    w_val = w_up.reshape(RANK, heads, NOPE + VDIM)[:, :, NOPE:]
    out = jnp.einsum("thr,rhv->thv", mixed, w_val, preferred_element_type=jnp.float32)
    return out.astype(jnp.bfloat16).reshape(mixed.shape[0], heads * VDIM)


def combine_parts(first, second):
    top = jnp.maximum(first[0], second[0])
    ratio_a = jnp.exp(first[0] - top)
    ratio_b = jnp.exp(second[0] - top)
    return (
        top,
        first[1] * ratio_a + second[1] * ratio_b,
        first[2] * ratio_a[..., None] + second[2] * ratio_b[..., None],
    )


def on_device(
    prompt_states, decode_states, lengths, page_table, w_query, w_down, kv_gain, w_up, w_out
):
    tok = prompt_states.shape[0]
    width = RANK + ROPE
    ctx_pos = lax.axis_index("ctx")
    ctx_count = lax.axis_size("ctx")
    index = ctx_pos * tok + jnp.arange(tok, dtype=jnp.int32)
    tenant, place = token_info(index, lengths)
    latent = latent_of(prompt_states, w_down, kv_gain, place.astype(jnp.float32))
    query = queries(prompt_states, w_query, w_up, place.astype(jnp.float32))
    heads = query.shape[1]
    pages_dev = tok // PAGE
    total_pages = page_table.shape[0]
    physical = ctx_pos * pages_dev + jnp.arange(pages_dev, dtype=jnp.int32)
    owned = jnp.sum(
        jnp.where(
            page_table[None, :] == physical[:, None],
            jnp.arange(total_pages, dtype=jnp.int32)[None, :],
            0,
        ),
        1,
    )
    slot_rows = (owned[:, None] * PAGE + jnp.arange(PAGE, dtype=jnp.int32)[None, :]).reshape(-1)
    piece = lax.all_gather(latent, "ctx", axis=0, tiled=True)
    top = jnp.full((tok, heads), FAR_LOW, jnp.float32)
    count = piece.shape[0]
    key_index = jnp.arange(count, dtype=jnp.int32)
    key_tenant, unused = token_info(key_index, lengths)
    mask = (key_tenant[None, :] == tenant[:, None]) & (key_index[None, :] <= index[:, None])
    score = jnp.einsum("thk,ck->thc", query, piece, preferred_element_type=jnp.float32)
    score = jnp.where(mask[:, None, :], score, FAR_LOW)
    new_top = jnp.maximum(top, jnp.max(score, -1))
    prob = jnp.where(mask[:, None, :], jnp.exp(score - new_top[..., None]), 0.0)
    new_total = jnp.sum(prob, -1)
    new_acc = jnp.einsum(
        "thc,cr->thr",
        prob.astype(jnp.bfloat16),
        piece[:, :RANK],
        preferred_element_type=jnp.float32,
    )
    mixed = (new_acc / new_total[..., None]).astype(jnp.bfloat16)
    heads_out = values_of(mixed, w_up)
    prefill_out = lax.psum_scatter(
        jnp.dot(heads_out, w_out, preferred_element_type=jnp.float32).astype(jnp.bfloat16),
        "head",
        scatter_dimension=0,
        tiled=True,
    )
    shifts = page_table[:pages_dev] // pages_dev
    stacked = latent.reshape(pages_dev, PAGE, width)
    for bit in range((ctx_count - 1).bit_length()):
        moved = from_behind(stacked, "ctx", 1 << bit)
        chosen = shifts // (1 << bit) % 2 == 1
        stacked = jnp.where(chosen[:, None, None], moved, stacked)
    paged_cache = stacked.reshape(pages_dev * PAGE, width)
    requests = decode_states.shape[0]
    dplace = lengths.astype(jnp.float32)
    new_key = latent_of(decode_states, w_down, kv_gain, dplace)
    dquery = queries(decode_states, w_query, w_up, dplace)
    key_tenant, unused = token_info(slot_rows, lengths)
    dmask = key_tenant[None, :] == jnp.arange(requests, dtype=jnp.int32)[:, None]
    score = jnp.einsum("qhk,ck->qhc", dquery, paged_cache, preferred_element_type=jnp.float32)
    score = jnp.where(dmask[:, None, :], score, FAR_LOW)
    top = jnp.max(score, -1)
    prob = jnp.where(dmask[:, None, :], jnp.exp(score - top[..., None]), 0.0)
    total = jnp.sum(prob, -1)
    acc = jnp.einsum(
        "qhc,cr->qhr",
        prob.astype(jnp.bfloat16),
        paged_cache[:, :RANK],
        preferred_element_type=jnp.float32,
    )
    top, total, acc = combined_all((top, total, acc), "ctx", combine_parts)
    own = jnp.einsum("qhk,qk->qh", dquery, new_key, preferred_element_type=jnp.float32)
    best = jnp.maximum(top, own)
    ratio = jnp.exp(top - best)
    pown = jnp.exp(own - best)
    total = total * ratio + pown
    acc = acc * ratio[..., None] + pown.astype(jnp.bfloat16).astype(jnp.float32)[
        ..., None
    ] * new_key[:, None, :RANK].astype(jnp.float32)
    dmixed = (acc / total[..., None]).astype(jnp.bfloat16)
    dheads = values_of(dmixed, w_up)
    partial_out = jnp.dot(dheads, w_out, preferred_element_type=jnp.float32)
    decode_out = lax.psum(partial_out.astype(jnp.bfloat16), "head")
    return (prefill_out, paged_cache, decode_out)


def solution(mesh):
    in_specs = (
        P("ctx", None),
        P(),
        P(),
        P(),
        P(None, "head"),
        P(),
        P(),
        P(None, "head"),
        P("head", None),
    )
    out_specs = (P(("ctx", "head"), None), P("ctx", None), P())
    return jax.shard_map(
        on_device, mesh=mesh, in_specs=in_specs, out_specs=out_specs, check_vma=False
    )
```

profile of v0, /device:TPU:1, one launch (start us, length us, event | category | flops | bytes accessed | tf_op | source)
XLA Modules:
  0.0 277.0 jit_solution(17890841127927537144)
XLA Ops:
  7.3 1.0 reduce-window.8
  8.2 1.3 fusion.51
  9.5 0.8 select_reduce_fusion.2
  10.4 0.7 convert_reduce_fusion.1
  11.2 0.5 copy-done.12
  11.7 3.0 %fusion.53 = f32[512,576]{0,1:T(8,128)S(1)} fusion(bf16[512,2048]{1,0:T(8,128)(2,1)} %param.11, bf16[2048,576]{0,1:T(8,128)(2,1)S(1)} %copy-done), kind=kOutput, calls=%fused_computation.147 | convolution fusion | flops 1207959552 | bytes 5636096 | tf_op jit(solution)/shard_map/dot_general | solution.py:61
  14.9 1.0 multiply_cosine_fusion
  16.0 0.9 pad_maximum_fusion
  17.4 2.5 collective-permute-start
  19.9 2.3 convolution_convert_fusion.4
  22.2 1.4 reshape.321
  23.6 0.7 fusion.54
  24.8 4.9 %fusion.7 = pred[512,8192]{1,0:T(8,128)(4,1)} fusion(s32[512]{0:T(512)S(1)} %copy-done.11, s32[8192]{0:T(1024)S(1)} %convert_reduce_fusion, s32[512]{0:T(512)S(1)} %copy-done.13), kind=kLoop, calls=%fused_computation.15 | loop fusion | flops 12582912 | bytes 4231168 | tf_op jit(solution)/shard_map/and | solution.py:129
  29.9 8.1 %collective-permute-done = bf16[4,128,576]{1,0,2:T(4,128)(2,1)S(1)} collective-permute-done((bf16[4,128,576]{1,0,2:T(4,128)(2,1)S(1)}, bf16[4,128,576]{1,0,2:T(4,128)(2,1)S(1)}, u32[]{:S(2)}, u32[]{:S(2)}) %collective-permute-start) | collective-permute-done | bytes 589856 | tf_op jit(solution)/shard_map/ppermute | solution.py:20
  39.1 19.9 %collective-permute-done.1 = bf16[4,128,576]{1,0,2:T(4,128)(2,1)S(1)} collective-permute-done((bf16[4,128,576]{1,0,2:T(4,128)(2,1)S(1)}, bf16[4,128,576]{1,0,2:T(4,128)(2,1)S(1)}, u32[]{:S(2)}, u32[]{:S(2)}) %collective-permute-start.1) | collective-permute-done | bytes 589856 | tf_op jit(solution)/shard_map/ppermute | solution.py:20
  59.6 3.1 %convolution_convert_fusion.2 = bf16[512,384]{0,1:T(8,128)(2,1)S(1)} fusion(bf16[512,2048]{1,0:T(8,128)(2,1)} %param.11, bf16[2048,384]{1,0:T(8,128)(2,1)} %param.15), kind=kOutput, calls=%fused_computation.26 | convolution fusion | flops 805502976 | bytes 4063232 | tf_op jit(solution)/shard_map/dot_general | solution.py:71
  62.8 9.8 %collective-permute-done.2 = bf16[4,128,576]{1,0,2:T(4,128)(2,1)S(1)} collective-permute-done((bf16[4,128,576]{1,0,2:T(4,128)(2,1)S(1)}, bf16[4,128,576]{1,0,2:T(4,128)(2,1)S(1)}, u32[]{:S(2)}, u32[]{:S(2)}) %collective-permute-start.2) | collective-permute-done | bytes 589856 | tf_op jit(solution)/shard_map/ppermute | solution.py:20
  73.3 1.8 convolution_bitcast_fusion
  75.0 22.2 %collective-permute-done.3 = bf16[4,128,576]{1,0,2:T(4,128)(2,1)S(1)} collective-permute-done((bf16[4,128,576]{1,0,2:T(4,128)(2,1)S(1)}, bf16[4,128,576]{1,0,2:T(4,128)(2,1)S(1)}, u32[]{:S(2)}, u32[]{:S(2)}) %collective-permute-start.3) | collective-permute-done | bytes 589856 | tf_op jit(solution)/shard_map/ppermute | solution.py:20
  97.6 0.9 copy.82
  98.5 1.1 copy.92
  100.3 23.8 %all-gather.2 = f32[64,2,512]{2,1,0:T(2,128)S(1)} all-gather(f32[4,2,512]{2,1,0:T(2,128)S(1)} %fusion.17), channel_id=4, replica_groups=mesh['ctx'=16,'head'=8] {'ctx'}, dimensions={0}, use_global_device_ids=true | all-gather | bytes 278528 | tf_op jit(solution)/shard_map/all_gather | solution.py:24
  124.2 15.8 %all-gather.3 = f32[16,4,2]{1,2,0:T(2,128)S(1)} all-gather(f32[1,4,2]{1,2,0:T(2,128)S(1)} %bitcast.103), channel_id=2, replica_groups=mesh['ctx'=16,'head'=8] {'ctx'}, dimensions={0}, use_global_device_ids=true | all-gather | bytes 544 | tf_op jit(solution)/shard_map/all_gather | solution.py:24
  139.9 17.5 %all-gather.4 = f32[16,4,2]{1,2,0:T(2,128)S(1)} all-gather(f32[1,4,2]{1,2,0:T(2,128)S(1)} %bitcast.106), channel_id=3, replica_groups=mesh['ctx'=16,'head'=8] {'ctx'}, dimensions={0}, use_global_device_ids=true | all-gather | bytes 544 | tf_op jit(solution)/shard_map/all_gather | solution.py:24
  157.5 23.3 %select_reduce_fusion = (f32[512,2]{0,1:T(2,128)S(1)}, f32[512,2,8192]{2,0,1:T(8,128)}) fusion(pred[512,8192]{1,0:T(8,128)(4,1)} %fusion.7, bf16[8192,576]{0,1:T(8,128)(2,1)} %all-gather.7.cloned.1.call-done, f32[512,2,32]{0,2,1:T(8,128)S(1)} %get-tuple-element.103, f32[512,2,32]{0,2,1:T(8,128)S(1)} %get-tuple-element.102, ...), kind=kOutput, calls=%fused_computation.10 | convolution fusion | flops 9682811904 | bytes 49549312 | tf_op jit(solution)/shard_map/thk,ck->thc/dot_general | solution.py:130
  180.8 15.6 %fusion.3 = f32[512,2]{0,1:T(2,128)S(1)} fusion(f32[512,2,8192]{2,0,1:T(8,128)} %get-tuple-element.123, f32[512,2]{0,1:T(2,128)S(1)} %broadcast_maximum_fusion, pred[512,8192]{1,0:T(8,128)(4,1)S(1)} %copy-done.2), kind=kLoop, calls=%fused_computation.11 | loop fusion | flops 33553408 | bytes 37756928 | tf_op jit(solution)/shard_map/reduce_sum | solution.py:134
  196.5 19.1 %divide_convert_fusion = bf16[512,2,512]{2,0,1:T(8,128)(2,1)S(1)} fusion(bf16[8192,576]{0,1:T(8,128)(2,1)} %all-gather.7.cloned.1.call-done, f32[512,2,8192]{2,0,1:T(8,128)} %get-tuple-element.123, f32[512,2]{0,1:T(2,128)S(1)} %broadcast_maximum_fusion, pred[512,8192]{1,0:T(8,128)(4,1)} %fusion.7, f32[512,2]{0,1:T(2,128)S(1)} %fusion.3), kind=kOutput, calls=%fused_computation.24 | convolution fusion | flops 8624537600 | bytes 47194112 | tf_op jit(solution)/shard_map/thc,cr->thr/dot_general | solution.py:135
  216.1 3.5 %convolution_convert_fusion = bf16[512,2048]{1,0:T(8,128)(2,1)} fusion(bf16[512,256]{0,1:T(8,128)(2,1)S(1)} %bitcast.99, bf16[256,2048]{1,0:T(8,128)(2,1)} %param.19), kind=kOutput, calls=%fused_computation.20 | convolution fusion | flops 537919488 | bytes 3407872 | tf_op jit(solution)/shard_map/dot_general | solution.py:144
  219.6 4.7 %while.14 = (s32[]{:T(128)}, f32[4,2]{0,1:T(2,128)S(1)}, f32[4,2]{0,1:T(2,128)S(1)}, f32[4,2,512]{2,1,0:T(2,128)S(1)}, f32[15,4,2]{1,2,0:T(2,128)S(1)}, /*index=...) while((s32[]{:T(128)}, f32[4,2]{0,1:T(2,128)S(1)}, f32[4,2]{0,1:T(2,128)S(1)}, ...), condition=%wide.region_13.14_spmd, body=%wide.region_12.13_spmd.sunk | while | flops 12338 | bytes 49701 | solution.py:27
  224.8 1.6 convolution_convert_fusion.1
  226.4 40.8 %psum.7 = bf16[4,2048]{1,0:T(4,128)(2,1)} all-reduce(bf16[4,2048]{1,0:T(4,128)(2,1)S(1)} %convolution_convert_fusion.1), channel_id=1, replica_groups=mesh['ctx'=16,'head'=8] {'head'}, use_global_device_ids=true, to_apply=%region_15.16 | all-reduce | flops 8192 | bytes 32768 | tf_op jit(solution)/shard_map/psum | solution.py:185
  267.2 3.0 %reduce-scatter.2.cloned.1.call-done = bf16[64,2048]{1,0:T(8,128)(2,1)} async-done(((bf16[512,2048]{1,0:T(8,128)(2,1)}), bf16[64,2048]{1,0:T(8,128)(2,1)}) %reduce-scatter.2.cloned.1.call-update) | async-done | bytes 262160 | tf_op jit(solution)/shard_map/reduce_scatter | solution.py:143
  (174 shorter events, 10.5 us)
Async XLA Ops:
  7.2 4.5 %copy-start = (bf16[2048,576]{0,1:T(8,128)(2,1)S(1)}, bf16[2048,576]{0,1:T(8,128)(2,1)}, u32[]{:S(2)}) copy-start(bf16[2048,576]{0,1:T(8,128)(2,1)} %param.16) | copy-start | bytes 7077892
  7.2 150.3 %all-gather.7.cloned.1.call-start = ((), (), s32[]{:S(2)}) async-start(), calls=%async_computation.1 | async-start | bytes 10027008 | tf_op jit(solution)/shard_map/all_gather | solution.py:124
  7.2 7.6 %copy-start.19 = (f32[32]{0:T(128)}, f32[32]{0:T(128)S(1)}, u32[]{:S(2)}) copy-start(f32[32]{0:T(128)S(1)} %negate_power_fusion) | copy-start | bytes 388
  8.2 6.5 %copy-start.17 = (s32[4,1]{0,1:T(1,128)}, s32[4,1]{0,1:T(1,128)S(1)}, u32[]{:S(2)}) copy-start(s32[4,1]{0,1:T(1,128)S(1)} %reduce-window.8) | copy-start | bytes 52
  11.7 4.2 %copy-start.14 = (f32[512]{0:T(512)S(1)}, f32[512]{0:T(512)}, u32[]{:S(2)}) copy-start(f32[512]{0:T(512)} %param.17) | copy-start | bytes 6148
  16.0 3.9 %copy-start.7 = (bf16[4,2048]{1,0:T(4,128)(2,1)S(1)}, bf16[4,2048]{1,0:T(4,128)(2,1)}, u32[]{:S(2)}) copy-start(bf16[4,2048]{1,0:T(4,128)(2,1)} %param.12) | copy-start | bytes 49156
  16.9 253.2 %reduce-scatter.2.cloned.1.call-start = ((), (), s32[]{:S(2)}) async-start(), calls=%async_computation.2 | async-start | bytes 2359296 | tf_op jit(solution)/shard_map/reduce_scatter | solution.py:143
  17.4 20.6 %collective-permute-start = (bf16[4,128,576]{1,0,2:T(4,128)(2,1)S(1)}, bf16[4,128,576]{1,0,2:T(4,128)(2,1)S(1)}, u32[]{:S(2)}, u32[]{:S(2)}) collective-permute-start(bf16[4,128,576]{1,0,2:T(4,128)(2,1)S(1)} %constant_dynamic-update-slice_fusion), channel_id=1, source_target_pairs={{120,0},{0,8},{8,16},{16,24},{24,32},{32,40},{40,48},{48,56},{56,6... | collective-permute-start | bytes 1769480 | tf_op jit(solution)/shard_map/ppermute | solution.py:20
  23.6 0.9 copy-start.18
  23.6 1.0 copy-start.22
  23.6 1.1 slice-start.3
  23.6 1.1 copy-start.11
  23.6 1.1 copy-start.13
  24.3 5.4 %copy-start.20 = (f32[32]{0:T(128)S(1)}, f32[32]{0:T(128)}, u32[]{:S(2)}) copy-start(f32[32]{0:T(128)} %copy-done.19) | copy-start | bytes 388
  24.3 5.4 %copy-start.21 = (f32[4]{0:T(128)S(1)}, f32[4]{0:T(128)}, u32[]{:S(2)}) copy-start(f32[4]{0:T(128)} %get-tuple-element.117) | copy-start | bytes 52
  24.3 5.5 %copy-start.15 = (f32[512]{0:T(512)S(1)}, f32[512]{0:T(512)}, u32[]{:S(2)}) copy-start(f32[512]{0:T(512)} %param.17) | copy-start | bytes 6148
  24.7 13.8 %copy-start.4 = (bf16[512,512]{1,0:T(8,128)(2,1)S(1)}, bf16[512,512]{1,0:T(8,128)(2,1)}, u32[]{:S(2)}) copy-start(bf16[512,512]{1,0:T(8,128)(2,1)} %param.18) | copy-start | bytes 1572868
  29.7 9.2 %slice-start.4 = ((bf16[4,2,192]{2,1,0:T(2,128)(2,1)}), bf16[4,2,128]{2,1,0:T(2,128)(2,1)S(1)}, s32[]{:S(2)}) async-start(bf16[4,2,192]{2,1,0:T(2,128)(2,1)} %reshape.321), calls=%async_computation.7 | async-start | bytes 4096 | tf_op jit(solution)/shard_map/slice | solution.py:76
  38.4 20.6 %collective-permute-start.1 = (bf16[4,128,576]{1,0,2:T(4,128)(2,1)S(1)}, bf16[4,128,576]{1,0,2:T(4,128)(2,1)S(1)}, u32[]{:S(2)}, u32[]{:S(2)}) collective-permute-start(bf16[4,128,576]{1,0,2:T(4,128)(2,1)S(1)} %broadcast_select_fusion), channel_id=1, source_target_pairs={{112,0},{120,8},{0,16},{8,24},{16,32},{24,40},{32,48},{40,56},{48,... | collective-permute-start | bytes 1769480 | tf_op jit(solution)/shard_map/ppermute | solution.py:20
  59.4 13.1 %collective-permute-start.2 = (bf16[4,128,576]{1,0,2:T(4,128)(2,1)S(1)}, bf16[4,128,576]{1,0,2:T(4,128)(2,1)S(1)}, u32[]{:S(2)}, u32[]{:S(2)}) collective-permute-start(bf16[4,128,576]{1,0,2:T(4,128)(2,1)S(1)} %broadcast_select_fusion.1), channel_id=1, source_target_pairs={{96,0},{104,8},{112,16},{120,24},{0,32},{8,40},{16,48},{24,56},{32... | collective-permute-start | bytes 1769480 | tf_op jit(solution)/shard_map/ppermute | solution.py:20
  59.6 13.5 %copy-start.16 = (s32[512]{0:T(512)S(1)}, s32[512]{0:T(512)}, u32[]{:S(2)}) copy-start(s32[512]{0:T(512)} %get-tuple-element.74) | copy-start | bytes 6148
  59.6 13.6 %copy-start.5 = (f32[512,32]{0,1:T(8,128)S(1)}, f32[512,32]{0,1:T(8,128)}, u32[]{:S(2)}) copy-start(f32[512,32]{0,1:T(8,128)} %get-tuple-element.110) | copy-start | bytes 196612
  59.6 13.6 %copy-start.6 = (f32[512,32]{0,1:T(8,128)S(1)}, f32[512,32]{0,1:T(8,128)}, u32[]{:S(2)}) copy-start(f32[512,32]{0,1:T(8,128)} %get-tuple-element.111) | copy-start | bytes 196612
  72.9 24.3 %collective-permute-start.3 = (bf16[4,128,576]{1,0,2:T(4,128)(2,1)S(1)}, bf16[4,128,576]{1,0,2:T(4,128)(2,1)S(1)}, u32[]{:S(2)}, u32[]{:S(2)}) collective-permute-start(bf16[4,128,576]{1,0,2:T(4,128)(2,1)S(1)} %broadcast_select_fusion.2), channel_id=1, source_target_pairs={{64,0},{72,8},{80,16},{88,24},{96,32},{104,40},{112,48},{120,56},{... | collective-permute-start | bytes 1769480 | tf_op jit(solution)/shard_map/ppermute | solution.py:20
  124.1 56.7 %copy-start.3 = (f32[64,2,512]{2,1,0:T(2,128)}, f32[64,2,512]{2,1,0:T(2,128)S(1)}, u32[]{:S(2)}) copy-start(f32[64,2,512]{2,1,0:T(2,128)S(1)} %all-gather.2) | copy-start | bytes 786436
  139.9 40.9 %copy-start.8 = (f32[16,4,2]{1,2,0:T(2,128)}, f32[16,4,2]{1,2,0:T(2,128)S(1)}, u32[]{:S(2)}) copy-start(f32[16,4,2]{1,2,0:T(2,128)S(1)} %all-gather.3) | copy-start | bytes 1540
  157.4 23.4 %copy-start.9 = (f32[16,4,2]{1,2,0:T(2,128)}, f32[16,4,2]{1,2,0:T(2,128)S(1)}, u32[]{:S(2)}) copy-start(f32[16,4,2]{1,2,0:T(2,128)S(1)} %all-gather.4) | copy-start | bytes 1540
  157.5 23.4 %copy-start.2 = (pred[512,8192]{1,0:T(8,128)(4,1)S(1)}, pred[512,8192]{1,0:T(8,128)(4,1)}, u32[]{:S(2)}) copy-start(pred[512,8192]{1,0:T(8,128)(4,1)} %fusion.7) | copy-start | bytes 12582916
  216.1 3.5 %slice-start = ((f32[64,2,512]{2,1,0:T(2,128)}), f32[60,2,512]{2,1,0:T(2,128)S(1)}, s32[]{:S(2)}) async-start(f32[64,2,512]{2,1,0:T(2,128)} %copy-done.3), calls=%async_computation.3 | async-start | bytes 491520 | tf_op jit(solution)/shard_map/slice | solution.py:26
  216.1 3.5 %slice-start.1 = ((f32[16,4,2]{1,2,0:T(2,128)}), f32[15,4,2]{1,2,0:T(2,128)S(1)}, s32[]{:S(2)}) async-start(f32[16,4,2]{1,2,0:T(2,128)} %copy-done.8), calls=%async_computation.4 | async-start | bytes 30720 | tf_op jit(solution)/shard_map/slice | solution.py:26
  216.1 3.5 %slice-start.2 = ((f32[16,4,2]{1,2,0:T(2,128)}), f32[15,4,2]{1,2,0:T(2,128)S(1)}, s32[]{:S(2)}) async-start(f32[16,4,2]{1,2,0:T(2,128)} %copy-done.9), calls=%async_computation.5 | async-start | bytes 30720 | tf_op jit(solution)/shard_map/slice | solution.py:26
  216.1 54.1 %copy-start.1 = (bf16[2048,576]{0,1:T(8,128)(2,1)S(1)}, bf16[2048,576]{0,1:T(8,128)(2,1)}, u32[]{:S(2)}) copy-start(bf16[2048,576]{0,1:T(8,128)(2,1)} %param.16) | copy-start | bytes 7077892
  (2 other events, 1.4 us)
Sparse Core Ops, SparseCore 0:
  17.0 111.1 all-gather.6
  219.7 50.4 reduce-scatter.1
where the time goes:
time: 280 us; the launch traced here: 277 us
  blocking collectives  97.9 us (35%)
  waiting for transfers between devices  63.1 us (23%)
  matrix products  59.7 us (21%)
  other arithmetic  31 us (11%)
  between operations  14.5 us (5%)
  local copies, waits for them, and re-layouts  7.63 us (3%)
  starting transfers between devices  2.92 us (1%)
    ppermute x4, waiting for transfers between devices, from_behind(): return lax.ppermute(block, axis, route)  60 us
    all_gather x3, blocking collectives, combined_all(): pieces = jax.tree.map(lambda part: lax.all_gather(part, axis), value)  57.1 us
    psum x1, blocking collectives, on_device(): decode_out = lax.psum(partial_out.astype(jnp.bfloat16), 'head')  40.8 us
    dot_general x1, matrix products, on_device(): jnp.einsum('thk,ck->thc', query, piece, preferred_element_type=jnp.float32)  23.3 us
    dot_general x1, matrix products, on_device(): jnp.einsum('thc,cr->thr', prob.astype(jnp.bfloat16), piece[:, :RANK], pre...  19.1 us
    reduce_sum x1, other arithmetic, on_device(): new_total = jnp.sum(prob, -1)  15.6 us
  transfers between devices with their start and end apart: 6, of which 5 were waited for; matrix products, arithmetic and copies ran while one was open for 10% of the time, Pallas kernels for 0%

commit v1 on v0

v1 whole, which is shorter than its diff:
```python
import functools
import math

import jax
import jax.numpy as jnp
import numpy as np
from jax import lax
from jax.experimental import pallas as pl
from jax.experimental.pallas import tpu as pltpu
from jax.sharding import PartitionSpec as P

NOPE = 128
ROPE = 64
VDIM = 128
RANK = 512
PAGE = 128
PAGES_DEV = 4
ROPE_BASE = 50000.0
HIDDEN = -3e38
FLOOR = -1e30
KAPPA = (NOPE + ROPE) ** -0.5 * math.log2(math.e)
DIST = (1, 3, 2, 4)
FREQ = (
    ROPE_BASE ** (-(np.arange(ROPE // 2, dtype=np.float64) * 2.0 / ROPE))
).astype(np.float32)[:, None]
ATTEND_MIB = {"first": 14, "middle": 16, "last": 16}
EXTRA = 8

F32 = jnp.float32
BF16 = jnp.bfloat16
NT = (((1,), (1,)), ((), ()))


def whole():
    return pl.BlockSpec()


def smem():
    return pl.BlockSpec(memory_space=pltpu.SMEM)


def anywhere():
    return pl.BlockSpec(memory_space=pl.ANY)


def in_hbm(x):
    return pltpu.with_memory_space_constraint(x, pltpu.HBM)


def params(mib):
    return pltpu.CompilerParams(vmem_limit_bytes=mib << 20)


def place_of():
    head = lax.axis_index("head")
    return lax.axis_index("ctx"), head // 2, lax.rem(head, 2)


def back_of(chip):
    chip = lax.rem(chip, 4)
    return jnp.where(chip == 0, 1, jnp.where(chip == 1, 3, jnp.where(chip == 2, 2, 4)))


GROUPS = RANK // 128


def tokens_of(ref):
    return ref.shape[0] * 128 // (RANK + ROPE)


def latent_rows(ref):
    n = tokens_of(ref)
    return jnp.concatenate([ref[g * n : (g + 1) * n, :] for g in range(GROUPS)], 1)


def rotary_rows(ref):
    both = ref[GROUPS * tokens_of(ref) :, :]
    return jnp.concatenate([both[:, :ROPE], both[:, ROPE:]], 0)


def ends_of(lengths):
    e0 = lengths[0]
    e1 = e0 + lengths[1]
    return e0, e1, e1 + lengths[2]


def start_of(index, ends):
    e0, e1, e2 = ends
    return jnp.where(
        index >= e2, e2, jnp.where(index >= e1, e1, jnp.where(index >= e0, e0, 0))
    )


def normed(comp, gain):
    return comp * lax.rsqrt(jnp.mean(comp * comp, -1, keepdims=True) + 1e-06) * gain


def turn_table(place, freq):
    angle = freq * place
    cos, sin = jnp.cos(angle), jnp.sin(angle)
    return jnp.concatenate([cos, cos, -sin, sin], 0).T


def turned(v, cs):
    half = ROPE // 2
    other = jnp.concatenate([v[:, half:], v[:, :half]], 1)
    return v * cs[:, :ROPE] + other * cs[:, ROPE:]


def prompt_turns(lengths, freq, first, n):
    index = first + lax.broadcasted_iota(jnp.int32, (1, n), 1)
    place = (index - start_of(index, ends_of(lengths))).astype(F32)
    return turn_table(place, freq)


def latent_kernel(lengths, x, w, gain, freq, out, cs, acc):
    step = pl.program_id(0)
    n = x.shape[0]

    @pl.when(step == 0)
    def _():
        ctx, _, core = place_of()
        cs[...] = prompt_turns(lengths, freq[...], (2 * ctx + core) * n, n)

    part = lax.dot_general(x[...], w[...], NT, preferred_element_type=F32)

    @pl.when(step == 0)
    def _():
        acc[...] = part

    @pl.when(step > 0)
    def _():
        acc[...] += part

    @pl.when(step == pl.num_programs(0) - 1)
    def _():
        comp = normed(acc[:, :RANK], gain[...]).astype(BF16)
        for g in range(GROUPS):
            out[g * n : (g + 1) * n, :] = comp[:, g * 128 : (g + 1) * 128]
        rot = turned(acc[:, RANK:], cs[...]).astype(BF16)
        out[GROUPS * n :, :] = jnp.concatenate([rot[: n // 2], rot[n // 2 :]], 1)


def latent_of(lengths, x, w_down_t, gain):
    tok, d = x.shape
    n = tok // 2
    width = w_down_t.shape[0]
    steps = 2
    return pl.pallas_call(
        latent_kernel,
        name="latent",
        grid=(steps,),
        in_specs=[
            smem(),
            pl.BlockSpec((n, d // steps), lambda i: (lax.rem(lax.axis_index("head"), 2), i)),
            pl.BlockSpec((width, d // steps), lambda i: (0, i)),
            pl.BlockSpec((1, RANK), lambda i: (0, 0)),
            pl.BlockSpec((ROPE // 2, 1), lambda i: (0, 0)),
        ],
        out_specs=pl.BlockSpec((n * width // 128, 128), lambda i: (0, 0)),
        out_shape=jax.ShapeDtypeStruct((n * width // 128, 128), BF16),
        scratch_shapes=[pltpu.VMEM((n, 2 * ROPE), F32), pltpu.VMEM((n, width), F32)],
        compiler_params=params(14),
        cost_estimate=pl.CostEstimate(
            flops=2 * n * d * width, bytes_accessed=4 << 20, transcendentals=0
        ),
    )(lengths, in_hbm(x), in_hbm(w_down_t), gain, FREQ)


def query_kernel(lengths, x, w, freq, _, out, cs, acc):
    step = pl.program_id(0)
    tok = x.shape[0]

    @pl.when(step == 0)
    def _():
        ctx, _, _ = place_of()
        cs[...] = prompt_turns(lengths, freq[...], ctx * tok, tok)

    part = jnp.dot(x[...], w[...], preferred_element_type=F32)

    @pl.when(step == 0)
    def _():
        acc[...] = part

    @pl.when(step > 0)
    def _():
        acc[...] += part

    @pl.when(step == pl.num_programs(0) - 1)
    def _():
        for h in range(2):
            at = h * (NOPE + ROPE)
            out[h, :, :NOPE] = (acc[:, at : at + NOPE] * KAPPA).astype(BF16)
            r = turned(acc[:, at + NOPE : at + NOPE + ROPE], cs[...]) * KAPPA
            out[h, :, NOPE:] = jnp.concatenate([r, jnp.zeros_like(r)], 1).astype(BF16)


def query_of(lengths, x, w_query, after):
    tok, d = x.shape
    width = w_query.shape[1]
    steps = 2
    return pl.pallas_call(
        query_kernel,
        name="query",
        grid=(steps,),
        in_specs=[
            smem(),
            pl.BlockSpec((tok, d // steps), lambda i: (0, i)),
            pl.BlockSpec((d // steps, width), lambda i: (i, 0)),
            pl.BlockSpec((ROPE // 2, 1), lambda i: (0, 0)),
            anywhere(),
        ],
        out_specs=pl.BlockSpec((2, tok, 256), lambda i: (0, 0, 0)),
        out_shape=jax.ShapeDtypeStruct((2, tok, 256), BF16),
        scratch_shapes=[pltpu.VMEM((tok, 2 * ROPE), F32), pltpu.VMEM((tok, width), F32)],
        compiler_params=params(14),
        cost_estimate=pl.CostEstimate(
            flops=1 << 20, bytes_accessed=1 << 16, transcendentals=0
        ),
    )(lengths, in_hbm(x), in_hbm(w_query), FREQ, after)


def decode_kernel(lengths, x, w_query, w_down_t, gain, freq, w_up, half, sib, out, self_out):
    n = tokens_of(half)
    tok = 2 * n
    rows = x.shape[0]
    keys = jnp.concatenate([latent_rows(half), latent_rows(sib)], 0)
    rot = jnp.concatenate([rotary_rows(half), rotary_rows(sib)], 0)
    ctx, _, core = place_of()
    lane = lax.broadcasted_iota(jnp.int32, (1, 128), 1)
    place = jnp.zeros((1, 128), jnp.int32)
    for r in range(rows):
        place = jnp.where(lane == r, lengths[r], place)
    cs = turn_table(place.astype(F32), freq[...])[:rows]
    lat = lax.dot_general(x[...], w_down_t[...], NT, preferred_element_type=F32)
    new_c = normed(lat[:, :RANK], gain[...]).astype(BF16)
    new_k = turned(lat[:, RANK:], cs).astype(BF16)
    q = jnp.dot(x[...], w_query[...], preferred_element_type=F32)
    index = lax.broadcasted_iota(jnp.int32, (rows, tok), 1)
    index = ctx * tok + jnp.where(index < n, index + core * n, index - core * n)
    tenant = sum((index >= e).astype(jnp.int32) for e in ends_of(lengths))
    mask = tenant == lax.broadcasted_iota(jnp.int32, (rows, tok), 0)
    for h in range(2):
        at = h * (NOPE + ROPE)
        wk = w_up[:, h * 256 : h * 256 + NOPE]
        wv = w_up[:, h * 256 + NOPE : h * 256 + 256]
        qn = (q[:, at : at + NOPE] * KAPPA).astype(BF16)
        qa = lax.dot_general(qn, wk, NT, preferred_element_type=F32).astype(BF16)
        qr = (turned(q[:, at + NOPE : at + NOPE + ROPE], cs) * KAPPA).astype(BF16)
        s = lax.dot_general(qa, keys, NT, preferred_element_type=F32)
        s = s + lax.dot_general(qr, rot, NT, preferred_element_type=F32)
        s = jnp.where(mask, s, HIDDEN)
        top = jnp.maximum(jnp.max(s, -1, keepdims=True), FLOOR)
        p = jnp.exp2(s - top)
        total = jnp.sum(p, -1, keepdims=True)
        mixed = jnp.dot(p.astype(BF16), keys, preferred_element_type=F32)
        part = jnp.dot(mixed.astype(BF16), wv, preferred_element_type=F32)
        own = jnp.sum(qa.astype(F32) * new_c.astype(F32), -1, keepdims=True)
        own = own + jnp.sum(qr.astype(F32) * new_k.astype(F32), -1, keepdims=True)
        to = slice(h * rows, h * rows + rows)
        mine = jnp.concatenate(
            [part, jnp.broadcast_to(top, (rows, 64)), jnp.broadcast_to(total, (rows, 64))], 1
        )
        for c in range(out.shape[0] // (2 * rows)):
            at = c * 2 * rows + h * rows
            out[at : at + rows, :] = mine
        self_out[to, :VDIM] = jnp.dot(new_c, wv, preferred_element_type=F32)
        self_out[to, VDIM : VDIM + 64] = jnp.broadcast_to(own, (rows, 64))
        self_out[to, VDIM + 64 :] = jnp.ones((rows, 64), F32)


def decode_partial(copies, lengths, x, w_query, w_down_t, gain, w_up, half, sib):
    rows = x.shape[0]
    return pl.pallas_call(
        decode_kernel,
        name="decode_partial",
        in_specs=[smem()] + [whole()] * 8,
        out_specs=[whole()] * 2,
        out_shape=[
            jax.ShapeDtypeStruct((copies * 2 * rows, 256), F32),
            jax.ShapeDtypeStruct((2 * rows, 256), F32),
        ],
        compiler_params=params(12),
        cost_estimate=pl.CostEstimate(
            flops=1 << 20, bytes_accessed=1 << 16, transcendentals=0
        ),
    )(lengths, x, w_query, w_down_t, gain, FREQ, w_up, half, sib)


def decode_merge_kernel(parts, own, w_out, _, out):
    rows = own.shape[0] // 2
    n = parts.shape[0] // own.shape[0]
    part = [parts[i * 2 * rows : (i + 1) * 2 * rows, :] for i in range(n)] + [own[...]]
    tops = [p[:, VDIM : VDIM + 1] for p in part]
    top = functools.reduce(jnp.maximum, tops)
    ratio = [jnp.exp2(t - top) for t in tops]
    total = sum(r * p[:, VDIM + 64 : VDIM + 65] for r, p in zip(ratio, part))
    acc = sum(r * p[:, :VDIM] for r, p in zip(ratio, part))
    heads = (acc / total).astype(BF16)
    got = jnp.dot(heads[:rows], w_out[:VDIM], preferred_element_type=F32)
    got = got + jnp.dot(heads[rows:], w_out[VDIM:], preferred_element_type=F32)
    out[...] = jnp.concatenate([got, jnp.zeros((EXTRA - rows, got.shape[1]), F32)], 0)


def decode_merge(parts, own, w_out, after):
    return pl.pallas_call(
        decode_merge_kernel,
        name="decode_merge",
        in_specs=[whole()] * 3 + [anywhere()],
        out_specs=whole(),
        out_shape=jax.ShapeDtypeStruct((EXTRA, w_out.shape[1]), F32),
        compiler_params=params(4),
        cost_estimate=pl.CostEstimate(
            flops=2 * 8 * 2048 * 256, bytes_accessed=2 << 20, transcendentals=0
        ),
    )(parts, own, w_out, after)


def attend_kernel(stage, places, lengths, q_own, q_sib, w_own, w_sib, *refs):
    nseg = len(places)
    segs, refs = refs[:nseg], refs[nseg:]
    if stage == "first":
        _, acc_out, rbuf, kbuf, vbuf, sbuf = refs
    elif stage == "middle":
        acc_in, _, acc_out, rbuf, kbuf, vbuf, sbuf = refs
    else:
        acc_in, _, mine, other, rbuf, kbuf, vbuf, sbuf, tile = refs
    tok = q_own.shape[1]
    heads = 4
    ctx, chip, core = place_of()
    base = ctx * tok
    ends = ends_of(lengths)
    row = base + lax.broadcasted_iota(jnp.int32, (tok, 128), 0)
    low = start_of(row, ends)
    blocks = []
    at = 0
    n = tokens_of(segs[0])
    for lat, place in zip(segs, places):
        if place is None:
            back = base + core * n
        else:
            back = base + core * n - (back_of(chip + place[0]) + place[1]) * tok
        rot = rotary_rows(lat)
        rbuf[at : at + n, :] = jnp.concatenate([rot, jnp.zeros_like(rot)], 1)
        blocks.append((lat, at, back, place is None))
        at += n
    ones = jnp.ones((n, 256 - VDIM), BF16)

    def expand(h):
        w = (w_own if h < 2 else w_sib)[:, (h % 2) * 256 : (h % 2) * 256 + 256]
        for lat, at, _, _ in blocks:
            kv = jnp.dot(latent_rows(lat), w, preferred_element_type=F32)
            kbuf[h, at : at + n, :] = kv[:, :NOPE].astype(BF16)
            vbuf[h, at : at + n, :] = kv[:, NOPE:].astype(BF16)

    def scores(h, block, top):
        _, at, back, causal = block
        q = q_own[h] if h < 2 else q_sib[h - 2]
        k = jnp.concatenate([kbuf[h, at : at + n, :], rbuf[at : at + n, :]], 1)
        s = lax.dot_general(q, k, NT, preferred_element_type=F32)
        for g in range(0, n, 128):
            key = back + g + lax.broadcasted_iota(jnp.int32, (1, 128), 1)
            mask = key >= low
            if causal:
                mask = mask & (key <= row)
            piece = jnp.where(mask, s[:, g : g + 128], HIDDEN)
            sbuf[h % 2, :, at + g : at + g + 128] = piece
            top = piece if top is None else jnp.maximum(top, piece)
        return top

    def finish(h, top, acc):
        if stage != "last":
            acc_out[h, :, : VDIM + 64] = acc[:, : VDIM + 64]
            acc_out[h, :, VDIM + 64 :] = jnp.broadcast_to(top, (tok, 64))
            return
        total = acc[:, VDIM:]
        some = total > 0
        safe = jnp.where(some, total, 1.0)
        tile[:, h * VDIM : h * VDIM + VDIM] = acc[:, :VDIM] / safe
        lse = jnp.where(some, top + jnp.log2(safe), HIDDEN)
        lane = lax.broadcasted_iota(jnp.int32, (tok, 128), 1)
        if h == 0:
            tile[:, heads * VDIM :] = lse
        else:
            tile[:, heads * VDIM :] = jnp.where(
                lane // 32 == h, lse, tile[:, heads * VDIM :]
            )

    expand(0)
    tops = None
    for block in blocks:
        tops = scores(0, block, tops)
    for h in range(heads):
        top = jnp.max(tops, -1, keepdims=True)
        tops = None
        if stage == "first":
            top = jnp.maximum(top, FLOOR)
            acc = None
        else:
            before = acc_in[h, :, VDIM + 64 : VDIM + 65]
            top = jnp.maximum(top, before)
            ratio = jnp.exp2(before - top)
            total = acc_in[h, :, VDIM : VDIM + 1] * ratio
            acc = jnp.concatenate(
                [acc_in[h, :, :VDIM] * ratio, jnp.broadcast_to(total, (tok, VDIM))], 1
            )
        if h + 1 < heads:
            expand(h + 1)
        for block in blocks:
            _, at, _, _ = block
            if h + 1 < heads:
                tops = scores(h + 1, block, tops)
            p = jnp.exp2(sbuf[h % 2, :, at : at + n] - top).astype(BF16)
            v = jnp.concatenate([vbuf[h, at : at + n, :], ones], 1)
            got = jnp.dot(p, v, preferred_element_type=F32)
            acc = got if acc is None else acc + got
        finish(h, top, acc)
    if stage == "last":
        part = tok // 8
        for i in range(4):
            to = slice(i * part, (i + 1) * part)
            at = (2 * i + core) * part
            mine[to, :] = tile[pl.ds(pl.multiple_of(at, part), part), :]
            at = (2 * i + 1 - core) * part
            other[to, :] = tile[pl.ds(pl.multiple_of(at, part), part), :]


def attend(stage, lengths, q_own, q_sib, w_own, w_sib, segs, places, state):
    _, tok, _ = q_own.shape
    heads = 4
    keys = tok // 2 * len(places)
    args = [lengths, q_own, q_sib, w_own, w_sib, *segs, *state]
    scratch = [
        pltpu.VMEM((keys, 128), BF16),
        pltpu.VMEM((heads, keys, 128), BF16),
        pltpu.VMEM((heads, keys, 128), BF16),
        pltpu.VMEM((2, tok, keys), F32),
    ]
    if stage == "last":
        width = heads * VDIM + 128
        out_shape = [jax.ShapeDtypeStruct((tok // 2, width), F32)] * 2
        scratch.append(pltpu.VMEM((tok, width), F32))
    else:
        out_shape = [jax.ShapeDtypeStruct((heads, tok, 256), F32)]
    return pl.pallas_call(
        functools.partial(attend_kernel, stage, places),
        name="attend_" + stage,
        in_specs=[smem()] + [whole()] * (len(args) - 2) + [anywhere()],
        out_specs=[whole()] * len(out_shape),
        out_shape=out_shape,
        scratch_shapes=scratch,
        compiler_params=params(ATTEND_MIB[stage]),
        cost_estimate=pl.CostEstimate(
            flops=2 * heads * tok * keys * 1024,
            bytes_accessed=8 << 20,
            transcendentals=heads * tok * keys,
        ),
    )(*args)


def merge_kernel(mine, came, w_own, w_sib, dec, _, out0, out1, out2, out3, heads):
    _, chip, _ = place_of()
    wide = 4 * VDIM
    for h in range(4):
        g = (h + 2) % 4
        la = mine[:, wide + h * 32 : wide + h * 32 + 1]
        lb = came[:, wide + g * 32 : wide + g * 32 + 1]
        top = jnp.maximum(la, lb)
        wa, wb = jnp.exp2(la - top), jnp.exp2(lb - top)
        scale = 1.0 / (wa + wb)
        o = mine[:, h * VDIM : h * VDIM + VDIM] * (wa * scale)
        o = o + came[:, g * VDIM : g * VDIM + VDIM] * (wb * scale)
        heads[:, h * VDIM : h * VDIM + VDIM] = o.astype(BF16)
    quarter = heads.shape[0] // 4
    part = jnp.concatenate(
        [
            heads[pl.ds(pl.multiple_of(lax.rem(chip + i, 4) * quarter, quarter), quarter), :]
            for i in range(4)
        ],
        0,
    )
    got = jnp.dot(part[:, : 2 * VDIM], w_own[...], preferred_element_type=F32)
    got = got + jnp.dot(part[:, 2 * VDIM :], w_sib[...], preferred_element_type=F32)
    for i, out in enumerate((out0, out1, out2, out3)):
        out[:quarter, :] = got[i * quarter : (i + 1) * quarter].astype(out.dtype)
        out[quarter:, :] = dec[...].astype(out.dtype)


def merge_out(mine, came, w_own, w_sib, dec, after):
    rows, d = mine.shape[0], w_own.shape[1]
    shapes = [
        jax.ShapeDtypeStruct((rows // 4 + EXTRA, d), F32 if i == 0 else BF16) for i in range(4)
    ]
    return pl.pallas_call(
        merge_kernel,
        name="merge_out",
        in_specs=[whole()] * 5 + [anywhere()],
        out_specs=[whole()] * 4,
        out_shape=shapes,
        scratch_shapes=[pltpu.VMEM((rows, 4 * VDIM), BF16)],
        compiler_params=params(24),
        cost_estimate=pl.CostEstimate(
            flops=2 * rows * 512 * d, bytes_accessed=5 << 20, transcendentals=0
        ),
    )(mine, came, w_own, w_sib, dec, after)


def sum_kernel(own, a, b, c, out, dec):
    rows = out.shape[0]
    got = own[...] + a[...].astype(F32) + b[...].astype(F32) + c[...].astype(F32)
    out[...] = got[:rows].astype(BF16)
    dec[...] = got[rows:]


def sum_parts(own, a, b, c):
    rows, d = own.shape
    return pl.pallas_call(
        sum_kernel,
        name="sum_parts",
        in_specs=[whole()] * 4,
        out_specs=[whole()] * 2,
        out_shape=[
            jax.ShapeDtypeStruct((rows - EXTRA, d), BF16),
            jax.ShapeDtypeStruct((EXTRA, d), F32),
        ],
        compiler_params=params(16),
        cost_estimate=pl.CostEstimate(
            flops=40_000_000_000, bytes_accessed=2 << 20, transcendentals=0
        ),
    )(own, a, b, c)


SLOT = RANK + PAGE


def shift_of(table, core, i):
    at = lax.div(table[2 * core + i], PAGES_DEV)
    return at


def pages_kernel(table, own, *refs):
    halves, (_, near, far) = refs[:8], refs[8:]
    _, chip, core = place_of()
    held = [(own, 0)]
    for i, half in enumerate(halves):
        held.append((half, back_of(chip + i % 4) + i // 4 * 4))

    def copy(half, i, out):
        n = tokens_of(half)
        for g in range(GROUPS):
            at = g * n + i * PAGE
            out[i * SLOT + g * PAGE : i * SLOT + (g + 1) * PAGE, :] = half[at : at + PAGE, :]
        rot = half[GROUPS * n :, :]
        if i:
            rot = jnp.concatenate([rot[:, ROPE:], rot[:, :ROPE]], 1)
        out[i * SLOT + RANK : (i + 1) * SLOT, :] = rot

    for i in range(PAGES_DEV // 2):
        shift = shift_of(table, core, i)
        for half, d in held:

            @pl.when(shift == d)
            def _(half=half, i=i):
                copy(half, i, near)

            @pl.when(shift - 8 == d)
            def _(half=half, i=i):
                copy(half, i, far)


def pages_of(table, own, halves, after):
    return pl.pallas_call(
        pages_kernel,
        name="pages",
        in_specs=[smem()] + [whole()] * 9 + [anywhere()],
        out_specs=[whole()] * 2,
        out_shape=[jax.ShapeDtypeStruct((PAGES_DEV // 2 * SLOT, 128), BF16)] * 2,
        compiler_params=params(16),
    )(table, own, *halves, after)


def choose_kernel(table, near, far, out):
    _, _, core = place_of()
    for i in range(PAGES_DEV // 2):
        rows = slice(i * SLOT, (i + 1) * SLOT)
        away = shift_of(table, core, i) > 8

        @pl.when(away)
        def _(rows=rows):
            out[rows, :] = far[rows, :]

        @pl.when(jnp.logical_not(away))
        def _(rows=rows):
            out[rows, :] = near[rows, :]


def choose(table, near, far):
    return pl.pallas_call(
        choose_kernel,
        name="choose",
        in_specs=[smem(), whole(), whole()],
        out_specs=whole(),
        out_shape=jax.ShapeDtypeStruct(near.shape, BF16),
        compiler_params=params(8),
    )(table, near, far)


def cache_kernel(own, came, out):
    _, _, core = place_of()
    tok = out.shape[1]
    for half, ref in ((core, own), (1 - core, came)):
        for i in range(PAGES_DEV // 2):
            at = pl.multiple_of(half * (tok // 2) + i * PAGE, PAGE)
            for g in range(GROUPS + 1):
                rows = slice(i * SLOT + g * PAGE, i * SLOT + (g + 1) * PAGE)
                page = ref[rows, :].astype(F32).T
                keep = min(PAGE, RANK + ROPE - g * PAGE)
                out[g * PAGE : g * PAGE + keep, pl.ds(at, PAGE)] = page[:keep].astype(BF16)


def cache_of(own, came, tok):
    return pl.pallas_call(
        cache_kernel,
        name="cache",
        in_specs=[whole(), whole()],
        out_specs=whole(),
        out_shape=jax.ShapeDtypeStruct((RANK + ROPE, tok), BF16),
        compiler_params=params(16),
    )(own, came).T


def on_device(
    prompt_states, decode_states, lengths, page_table, w_query, w_down, kv_gain, w_up, w_out
):
    n_ctx, n_head = lax.axis_size("ctx"), lax.axis_size("head")

    def over_ctx(block, dist_of):
        route = [
            (c * n_head + j, (c + dist_of(j)) % n_ctx * n_head + j)
            for c in range(n_ctx)
            for j in range(n_head)
        ]
        return lax.ppermute(block, ("ctx", "head"), route)

    def over_x(block, s):
        return lax.ppermute(block, "head", [(j, (j + 2 * s) % n_head) for j in range(n_head)])

    def to_sibling(block):
        return lax.ppermute(block, "head", [(j, j ^ 1) for j in range(n_head)])

    def chip_dist(j, k=0):
        return DIST[(j // 2 + k) % len(DIST)]

    gain = kv_gain[None, :]
    w_down_t = w_down.T
    w_up_sib = to_sibling(w_up)
    w_out_sib = to_sibling(w_out)
    half = latent_of(lengths, prompt_states, w_down_t, gain)
    near0 = over_ctx(half, chip_dist)
    half_sib = to_sibling(half)
    q_own = query_of(lengths, prompt_states, w_query, half_sib)
    q_sib = to_sibling(q_own)
    far0 = over_ctx(near0, lambda j: 4)
    near2 = over_ctx(near0, lambda j: chip_dist(j, 2) - chip_dist(j))
    near3 = over_x(near0, 1)
    near1 = over_x(near0, -1)
    far2 = over_ctx(far0, lambda j: chip_dist(j, 2) - chip_dist(j))
    far3 = over_x(far0, 1)
    far1 = over_x(far0, -1)

    dpart, dself = decode_partial(
        n_ctx, lengths, decode_states, w_query, w_down_t, gain, w_up, half, half_sib
    )
    parts = lax.all_to_all(dpart, "ctx", 0, 0, tiled=True)

    weights = (q_own, q_sib, w_up, w_up_sib)
    state = attend("first", lengths, *weights, [half, near0], (None, (0, 0)), [dpart])
    dec = decode_merge(parts, dself, w_out, dself)
    state = attend(
        "middle",
        lengths,
        *weights,
        [near2, near3, near1, far0],
        ((2, 0), (3, 0), (1, 0), (0, 4)),
        (*state, dpart),
    )
    mine, other = attend(
        "last", lengths, *weights, [far2, far3, far1], ((2, 4), (3, 4), (1, 4)), (*state, dec)
    )
    came = to_sibling(other)
    halves = [near0, near1, near2, near3, far0, far1, far2, far3]
    page_near, page_far = pages_of(page_table, half, halves, mine)
    out0, out1, out2, out3 = merge_out(mine, came, w_out, w_out_sib, dec, page_near)
    got1 = over_x(out1, 1)
    got3 = over_x(out3, -1)
    got2 = over_x(out2, 2)
    prefill_out, dec = sum_parts(out0, got1, got2, got3)
    decode_out = (dec + to_sibling(dec))[: decode_states.shape[0]].astype(BF16)

    page = choose(page_table, page_near, over_ctx(page_far, lambda j: 8))
    paged_cache = cache_of(page, to_sibling(page), prompt_states.shape[0])
    return (prefill_out, paged_cache, decode_out)


def solution(mesh):
    in_specs = (
        P("ctx", None),
        P(),
        P(),
        P(),
        P(None, "head"),
        P(),
        P(),
        P(None, "head"),
        P("head", None),
    )
    out_specs = (P(("ctx", "head"), None), P("ctx", None), P())
    return jax.shard_map(
        on_device, mesh=mesh, in_specs=in_specs, out_specs=out_specs, check_vma=False
    )
```

time: 280 us -> 86.7 us (0.31)
  blocking collectives: 97.9 us -> 0 us
  matrix products: 59.7 us -> 0 us
  waiting for transfers between devices: 63.1 us -> 21.8 us
  Pallas kernels: 0 us -> 33.2 us
  other arithmetic: 31 us -> 0.61 us
  starting transfers between devices: 2.92 us -> 27.8 us
  between operations: 14.5 us -> 0.78 us
  local copies, waits for them, and re-layouts: 7.63 us -> 2.09 us
    dot_general x14 -> x0, matrix products: 59.7 us -> none  [the longest x1 23.3 us: on_device(): jnp.einsum('thk,ck->thc', query, piece, preferred_element_type=jnp.float32)]
    all_gather x3 -> x0, blocking collectives: 57.1 us -> none  [combined_all(): pieces = jax.tree.map(lambda part: lax.all_gather(part, axis), value)]
    ppermute x4 -> x19, waiting for transfers between devices: 60 us -> 18.7 us  [the longest x5 10.4 us: over_ctx(): return lax.ppermute(block, ('ctx', 'head'), route)]
    psum x1 -> x0, blocking collectives: 40.8 us -> none  [on_device(): decode_out = lax.psum(partial_out.astype(jnp.bfloat16), 'head')]
    pallas_call x0 -> x12, Pallas kernels: none -> 33.2 us  [the longest x3 16.6 us: attend(): pl.pallas_call(functools.partial(attend_kernel, stage, places), name='att...]
    ppermute x4 -> x19, starting transfers between devices: 2.84 us -> 23.8 us  [the longest x7 10.4 us: over_x(): lax.ppermute(block, 'head', [(j, (j + 2 * s) % n_head) for j in range(n_h...]
    reduce_sum x7 -> x0, other arithmetic: 17.6 us -> none  [the longest x1 15.6 us: on_device(): new_total = jnp.sum(prob, -1)]
    and x1 -> x0, other arithmetic: 4.92 us -> none  [on_device(): (key_tenant[None, :] == tenant[:, None]) & (key_index[None, :] <= index[:...]
  transfers between devices with their start and end apart: 6 -> 20, of which waited for: 5 -> 8; matrix products, arithmetic and copies ran while one was open for 10% -> 0% of each run, Pallas kernels for 0% -> 35%
where the time goes in v1:
time: 86.7 us; the launch traced here: 86.3 us
  Pallas kernels  33.2 us (38%)
  starting transfers between devices  27.8 us (32%)
  waiting for transfers between devices  21.8 us (25%)
  local copies, waits for them, and re-layouts  2.09 us (2%)
    pallas_call x3, Pallas kernels, attend(): pl.pallas_call(functools.partial(attend_kernel, stage, places), name='att...  16.6 us
    ppermute x7, starting transfers between devices, over_x(): lax.ppermute(block, 'head', [(j, (j + 2 * s) % n_head) for j in range(n_h...  10.4 us
    ppermute x5, waiting for transfers between devices, over_ctx(): return lax.ppermute(block, ('ctx', 'head'), route)  10.4 us
    ppermute x7, starting transfers between devices, to_sibling(): return lax.ppermute(block, 'head', [(j, j ^ 1) for j in range(n_head)])  8.81 us
    ppermute x7, waiting for transfers between devices, over_x(): lax.ppermute(block, 'head', [(j, (j + 2 * s) % n_head) for j in range(n_h...  8.22 us
    ppermute x5, starting transfers between devices, over_ctx(): return lax.ppermute(block, ('ctx', 'head'), route)  4.53 us
    pallas_call x1, Pallas kernels, query_of(): pl.pallas_call(query_kernel, name='query', grid=(steps,), in_specs=[smem(...  4.16 us
    all_to_all x1, starting transfers between devices, on_device(): parts = lax.all_to_all(dpart, 'ctx', 0, 0, tiled=True)  4.04 us
  transfers between devices with their start and end apart: 20, of which 8 were waited for; matrix products, arithmetic and copies ran while one was open for 0% of the time, Pallas kernels for 35%

profile of v1, /device:TPU:1, one launch (start us, length us, event | category | flops | bytes accessed | tf_op | source)
XLA Modules:
  0.0 86.3 jit_solution(11955418856062471441)
XLA Ops:
  0.6 0.7 copy-done.4
  2.7 3.4 %latent.1.half.refs_0_.own = bf16[1152,128]{1,0:T(8,128)(2,1)S(1)} custom-call(s32[4]{0:T(128)S(1)} %copy-done.7, bf16[512,2048]{1,0:T(8,128)(2,1)} %x.4, bf16[576,2048]{1,0:T(8,128)(2,1)} %bitcast.5, f32[1,512]{1,0:T(1,128)S(1)} %bitcast.8, f32[32,1]{1,0:T(8,128)S(1)} %copy-done.4), custom_call_target="tpu_custom_call" | custom-call | flops 603979776 | bytes 4194304 | tf_op jit(solution)/shard_map/latent/pallas_call | solution.py:149
  6.1 1.5 %collective-permute-start = (bf16[1152,128]{1,0:T(8,128)(2,1)S(1)}, bf16[1152,128]{1,0:T(8,128)(2,1)S(1)}, u32[]{:S(2)}, u32[]{:S(2)}) collective-permute-start(bf16[1152,128]{1,0:T(8,128)(2,1)S(1)} %latent.1.half.refs_0_.own), channel_id=1, source_target_pairs={{0,1},{1,0},{2,3},{3,2},{4,5},{5,4},{6,7},{7,6},{8,9},{9,8},{10,11... | collective-permute-start | bytes 884744 | tf_op jit(solution)/shard_map/ppermute | solution.py:649
  7.7 1.7 %collective-permute-start.3 = (bf16[1152,128]{1,0:T(8,128)(2,1)S(1)}, bf16[1152,128]{1,0:T(8,128)(2,1)S(1)}, u32[]{:S(2)}, u32[]{:S(2)}) collective-permute-start(bf16[1152,128]{1,0:T(8,128)(2,1)S(1)} %latent.1.half.refs_0_.own), channel_id=1, source_target_pairs={{0,8},{1,9},{2,26},{3,27},{4,20},{5,21},{6,38},{7,39},{8,16},{9,17... | collective-permute-start | bytes 884744 | tf_op jit(solution)/shard_map/ppermute | solution.py:643
  9.4 4.2 %query.1.q_own = bf16[2,512,256]{2,1,0:T(8,128)(2,1)S(1)} custom-call(s32[4]{0:T(128)S(1)} %copy-done.7, bf16[512,2048]{1,0:T(8,128)(2,1)} %x.4, bf16[2048,384]{1,0:T(8,128)(2,1)} %w_query.1, f32[32,1]{1,0:T(8,128)S(1)} %copy-done.4, bf16[1152,128]{1,0:T(8,128)(2,1)S(1)} %collective-permute-done._.sib), custom_call_target="tpu_custom_call" | custom-call | flops 1048576 | bytes 65536 | tf_op jit(solution)/shard_map/query/pallas_call | solution.py:202
  13.6 0.8 collective-permute-start.1
  14.4 6.6 %collective-permute-done.3.refs_1_.refs_0_ = bf16[1152,128]{1,0:T(8,128)(2,1)S(1)} collective-permute-done((bf16[1152,128]{1,0:T(8,128)(2,1)S(1)}, bf16[1152,128]{1,0:T(8,128)(2,1)S(1)}, u32[]{:S(2)}, u32[]{:S(2)}) %collective-permute-start.3) | collective-permute-done | bytes 294944 | tf_op jit(solution)/shard_map/ppermute | solution.py:643
  21.1 3.4 %decode_partial.1 = (f32[128,256]{1,0:T(8,128)}, f32[8,256]{1,0:T(8,128)S(1)}) custom-call(s32[4]{0:T(128)S(1)} %copy-done.7, bf16[4,2048]{1,0:T(4,128)(2,1)S(1)} %copy-done.5, bf16[2048,384]{1,0:T(8,128)(2,1)S(1)} %copy-done.1, bf16[576,2048]{1,0:T(8,128)(2,1)S(1)} %bitcast.6, f32[1,512]{1,0:T(1,128)S(1)} %bitcast.9, f32[32,1]{1,0:T(8,128)S(1)} %copy-done.4, ...), custom_call_target="tpu_custom_call" | custom-call | flops 1048576 | bytes 65536 | tf_op jit(solution)/shard_map/decode_partial/pallas_call | solution.py:274
  24.5 4.0 %all-to-all-start = ((f32[16,8,256]{2,1,0:T(8,128)}), f32[16,8,256]{2,1,0:T(8,128)S(1)}, u32[]{:S(2)}, u32[]{:S(2)}) async-start(f32[16,8,256]{2,1,0:T(8,128)} %bitcast.2), calls=%async_computation | async-start | bytes 262144 | tf_op jit(solution)/shard_map/all_to_all | solution.py:674
  28.5 2.3 %collective-permute-start.10 = (bf16[1152,128]{1,0:T(8,128)(2,1)S(1)}, bf16[1152,128]{1,0:T(8,128)(2,1)S(1)}, u32[]{:S(2)}, u32[]{:S(2)}) collective-permute-start(bf16[1152,128]{1,0:T(8,128)(2,1)S(1)} %collective-permute-done.3.refs_1_.refs_0_), channel_id=1, source_target_pairs={{0,6},{1,7},{2,0},{3,1},{4,2},{5,3},{6,4},{7,5},{8,14},{9,15},{10,... | collective-permute-start | bytes 884744 | tf_op jit(solution)/shard_map/ppermute | solution.py:646
  30.8 1.3 %collective-permute-start.8 = (bf16[1152,128]{1,0:T(8,128)(2,1)S(1)}, bf16[1152,128]{1,0:T(8,128)(2,1)}, u32[]{:S(2)}, u32[]{:S(2)}) collective-permute-start(bf16[1152,128]{1,0:T(8,128)(2,1)S(1)} %collective-permute-done.3.refs_1_.refs_0_), channel_id=1, source_target_pairs={{0,8},{1,9},{2,10},{3,11},{4,124},{5,125},{6,126},{7,127},{8,16},{... | collective-permute-start | bytes 884744 | tf_op jit(solution)/shard_map/ppermute | solution.py:643
  32.1 3.1 %all-to-all-done = f32[16,8,256]{2,1,0:T(8,128)S(1)} async-done(((f32[16,8,256]{2,1,0:T(8,128)}), f32[16,8,256]{2,1,0:T(8,128)S(1)}, u32[]{:S(2)}, u32[]{:S(2)}) %all-to-all-start) | async-done | bytes 131104 | tf_op jit(solution)/shard_map/all_to_all | solution.py:674
  35.6 2.8 %collective-permute-start.12 = (bf16[256,2048]{1,0:T(8,128)(2,1)S(1)}, bf16[256,2048]{1,0:T(8,128)(2,1)S(1)}, u32[]{:S(2)}, u32[]{:S(2)}) collective-permute-start(bf16[256,2048]{1,0:T(8,128)(2,1)S(1)} %copy-done.2), channel_id=1, source_target_pairs={{0,1},{1,0},{2,3},{3,2},{4,5},{5,4},{6,7},{7,6},{8,9},{9,8},{10,11... | collective-permute-start | bytes 3145736 | tf_op jit(solution)/shard_map/ppermute | solution.py:649
  38.6 4.0 %attend_first.1.refs_4_ = f32[4,512,256]{2,1,0:T(8,128)S(1)} custom-call(s32[4]{0:T(128)S(1)} %copy-done.8, bf16[2,512,256]{2,1,0:T(8,128)(2,1)S(1)} %query.1.q_own, bf16[2,512,256]{2,1,0:T(8,128)(2,1)} %collective-permute-done.1.q_sib, bf16[512,512]{1,0:T(8,128)(2,1)S(1)} %copy-done.3, bf16[512,512]{1,0:T(8,128)(2,1)} %collective-permute-done.2.w_sib, ...), custom_call_target="tpu_custom_call" | custom-call | flops 2147483648 | bytes 8388608 | tf_op jit(solution)/shard_map/attend_first/pallas_call | solution.py:445
  42.6 2.8 %collective-permute-start.6 = (bf16[1152,128]{1,0:T(8,128)(2,1)S(1)}, bf16[1152,128]{1,0:T(8,128)(2,1)S(1)}, u32[]{:S(2)}, u32[]{:S(2)}) collective-permute-start(bf16[1152,128]{1,0:T(8,128)(2,1)S(1)} %collective-permute-done.4.refs_3_.refs_4_), channel_id=1, source_target_pairs={{0,2},{1,3},{2,4},{3,5},{4,6},{5,7},{6,0},{7,1},{8,10},{9,11},{10,... | collective-permute-start | bytes 884744 | tf_op jit(solution)/shard_map/ppermute | solution.py:646
  45.5 1.1 %collective-permute-start.7 = (bf16[1152,128]{1,0:T(8,128)(2,1)S(1)}, bf16[1152,128]{1,0:T(8,128)(2,1)S(1)}, u32[]{:S(2)}, u32[]{:S(2)}) collective-permute-start(bf16[1152,128]{1,0:T(8,128)(2,1)S(1)} %collective-permute-done.4.refs_3_.refs_4_), channel_id=1, source_target_pairs={{0,6},{1,7},{2,0},{3,1},{4,2},{5,3},{6,4},{7,5},{8,14},{9,15},{10,... | collective-permute-start | bytes 884744 | tf_op jit(solution)/shard_map/ppermute | solution.py:646
  46.6 6.4 %attend_middle.1.refs_3_ = f32[4,512,256]{2,1,0:T(8,128)S(1)} custom-call(s32[4]{0:T(128)S(1)} %copy-done.8, bf16[2,512,256]{2,1,0:T(8,128)(2,1)S(1)} %query.1.q_own, bf16[2,512,256]{2,1,0:T(8,128)(2,1)} %collective-permute-done.1.q_sib, bf16[512,512]{1,0:T(8,128)(2,1)S(1)} %copy-done.3, bf16[512,512]{1,0:T(8,128)(2,1)} %collective-permute-done.2.w_sib, ...), custom_call_target="tpu_custom_call" | custom-call | flops 4294967296 | bytes 8388608 | tf_op jit(solution)/shard_map/attend_middle/pallas_call | solution.py:445
  53.4 1.1 %collective-permute-done.7.refs_2_.refs_5_ = bf16[1152,128]{1,0:T(8,128)(2,1)S(1)} collective-permute-done((bf16[1152,128]{1,0:T(8,128)(2,1)S(1)}, bf16[1152,128]{1,0:T(8,128)(2,1)S(1)}, u32[]{:S(2)}, u32[]{:S(2)}) %collective-permute-start.7) | collective-permute-done | bytes 294944 | tf_op jit(solution)/shard_map/ppermute | solution.py:646
  54.5 6.1 %attend_last.1 = (f32[256,640]{1,0:T(8,128)S(1)}, f32[256,640]{1,0:T(8,128)S(1)}) custom-call(s32[4]{0:T(128)S(1)} %copy-done.8, bf16[2,512,256]{2,1,0:T(8,128)(2,1)S(1)} %query.1.q_own, bf16[2,512,256]{2,1,0:T(8,128)(2,1)} %collective-permute-done.1.q_sib, bf16[512,512]{1,0:T(8,128)(2,1)S(1)} %copy-done.3, bf16[512,512]{1,0:T(8,128)(2,1)} %collective-permute-done.2.w_sib, ...), custom_call_target="tpu_custom_call" | custom-call | flops 3221225472 | bytes 8388608 | tf_op jit(solution)/shard_map/attend_last/pallas_call | solution.py:445
  60.6 1.3 %collective-permute-start.11 = (f32[256,640]{1,0:T(8,128)S(1)}, f32[256,640]{1,0:T(8,128)S(1)}, u32[]{:S(2)}, u32[]{:S(2)}) collective-permute-start(f32[256,640]{1,0:T(8,128)S(1)} %get-tuple-element.18), channel_id=1, source_target_pairs={{0,1},{1,0},{2,3},{3,2},{4,5},{5,4},{6,7},{7,6},{8,9},{9,8},{10,11... | collective-permute-start | bytes 1966088 | tf_op jit(solution)/shard_map/ppermute | solution.py:649
  61.9 1.3 %pages.1 = (bf16[1280,128]{1,0:T(8,128)(2,1)S(1)}, bf16[1280,128]{1,0:T(8,128)(2,1)S(1)}) custom-call(s32[64]{0:T(128)S(1)} %copy-done.9, bf16[1152,128]{1,0:T(8,128)(2,1)S(1)} %latent.1.half.refs_0_.own, bf16[1152,128]{1,0:T(8,128)(2,1)S(1)} %collective-permute-done.3.refs_1_.refs_0_, bf16[1152,128]{1,0:T(8,128)(2,1)S(1)} %collective-permute-done.10.refs_2_.refs_1_, ...), custom_call_target="tpu_custom_call" | custom-call | tf_op jit(solution)/shard_map/pages/pallas_call | solution.py:572
  63.2 1.4 %collective-permute-start.16 = (bf16[1280,128]{1,0:T(8,128)(2,1)S(1)}, bf16[1280,128]{1,0:T(8,128)(2,1)S(1)}, u32[]{:S(2)}, u32[]{:S(2)}) collective-permute-start(bf16[1280,128]{1,0:T(8,128)(2,1)S(1)} %get-tuple-element.25), channel_id=1, source_target_pairs={{0,64},{1,65},{2,66},{3,67},{4,68},{5,69},{6,70},{7,71},{8,72},{9,... | collective-permute-start | bytes 983048 | tf_op jit(solution)/shard_map/ppermute | solution.py:643
  64.6 1.6 %merge_out.1 = (f32[72,2048]{1,0:T(8,128)S(1)}, bf16[72,2048]{1,0:T(8,128)(2,1)S(1)}, bf16[72,2048]{1,0:T(8,128)(2,1)S(1)}, bf16[72,2048]{1,0:T(8,128)(2,1)S(1)}) custom-call(f32[256,640]{1,0:T(8,128)S(1)} %get-tuple-element.17.refs_8_.mine, f32[256,640]{1,0:T(8,128)S(1)} %collective-permute-done.11.came, bf16[256,2048]{1,0:T(8,128)(2,1)S(1)} %copy-done.2, ...), custom_call_target="tpu_custom_call" | custom-call | flops 536870912 | bytes 5242880 | tf_op jit(solution)/shard_map/merge_out/pallas_call | solution.py:494
  66.2 1.5 %collective-permute-start.13 = (bf16[72,2048]{1,0:T(8,128)(2,1)S(1)}, bf16[72,2048]{1,0:T(8,128)(2,1)S(1)}, u32[]{:S(2)}, u32[]{:S(2)}) collective-permute-start(bf16[72,2048]{1,0:T(8,128)(2,1)S(1)} %get-tuple-element.21), channel_id=1, source_target_pairs={{0,2},{1,3},{2,4},{3,5},{4,6},{5,7},{6,0},{7,1},{8,10},{9,11},{10,... | collective-permute-start | bytes 884744 | tf_op jit(solution)/shard_map/ppermute | solution.py:646
  67.7 1.1 %collective-permute-start.14 = (bf16[72,2048]{1,0:T(8,128)(2,1)S(1)}, bf16[72,2048]{1,0:T(8,128)(2,1)S(1)}, u32[]{:S(2)}, u32[]{:S(2)}) collective-permute-start(bf16[72,2048]{1,0:T(8,128)(2,1)S(1)} %get-tuple-element.22), channel_id=1, source_target_pairs={{0,4},{1,5},{2,6},{3,7},{4,0},{5,1},{6,2},{7,3},{8,12},{9,13},{10,... | collective-permute-start | bytes 884744 | tf_op jit(solution)/shard_map/ppermute | solution.py:646
  68.8 1.5 %collective-permute-start.15 = (bf16[72,2048]{1,0:T(8,128)(2,1)S(1)}, bf16[72,2048]{1,0:T(8,128)(2,1)S(1)}, u32[]{:S(2)}, u32[]{:S(2)}) collective-permute-start(bf16[72,2048]{1,0:T(8,128)(2,1)S(1)} %get-tuple-element.23), channel_id=1, source_target_pairs={{0,6},{1,7},{2,0},{3,1},{4,2},{5,3},{6,4},{7,5},{8,14},{9,15},{10,... | collective-permute-start | bytes 884744 | tf_op jit(solution)/shard_map/ppermute | solution.py:646
  70.4 3.8 %collective-permute-done.16.far = bf16[1280,128]{1,0:T(8,128)(2,1)S(1)} collective-permute-done((bf16[1280,128]{1,0:T(8,128)(2,1)S(1)}, bf16[1280,128]{1,0:T(8,128)(2,1)S(1)}, u32[]{:S(2)}, u32[]{:S(2)}) %collective-permute-start.16) | collective-permute-done | bytes 327712 | tf_op jit(solution)/shard_map/ppermute | solution.py:643
  74.7 0.9 %collective-permute-start.17 = (bf16[1280,128]{1,0:T(8,128)(2,1)S(1)}, bf16[1280,128]{1,0:T(8,128)(2,1)S(1)}, u32[]{:S(2)}, u32[]{:S(2)}) collective-permute-start(bf16[1280,128]{1,0:T(8,128)(2,1)S(1)} %choose.1.own), channel_id=1, source_target_pairs={{0,1},{1,0},{2,3},{3,2},{4,5},{5,4},{6,7},{7,6},{8,9},{9,8},{10,11... | collective-permute-start | bytes 983048 | tf_op jit(solution)/shard_map/ppermute | solution.py:649
  75.8 6.2 %collective-permute-done.14.b = bf16[72,2048]{1,0:T(8,128)(2,1)S(1)} collective-permute-done((bf16[72,2048]{1,0:T(8,128)(2,1)S(1)}, bf16[72,2048]{1,0:T(8,128)(2,1)S(1)}, u32[]{:S(2)}, u32[]{:S(2)}) %collective-permute-start.14) | collective-permute-done | bytes 294944 | tf_op jit(solution)/shard_map/ppermute | solution.py:646
  82.3 0.8 sum_parts.1
  83.2 1.4 %collective-permute-start.18 = (f32[8,2048]{1,0:T(8,128)S(1)}, f32[8,2048]{1,0:T(8,128)S(1)}, u32[]{:S(2)}, u32[]{:S(2)}) collective-permute-start(f32[8,2048]{1,0:T(8,128)S(1)} %get-tuple-element.26), channel_id=1, source_target_pairs={{0,1},{1,0},{2,3},{3,2},{4,5},{5,4},{6,7},{7,6},{8,9},{9,8},{10,11... | collective-permute-start | bytes 196616 | tf_op jit(solution)/shard_map/ppermute | solution.py:649
  84.6 1.1 %cache.1 = bf16[576,512]{1,0:T(8,128)(2,1)} custom-call(bf16[1280,128]{1,0:T(8,128)(2,1)S(1)} %choose.1.own, bf16[1280,128]{1,0:T(8,128)(2,1)S(1)} %collective-permute-done.17.came), custom_call_target="tpu_custom_call" | custom-call | tf_op jit(solution)/shard_map/cache/pallas_call | solution.py:622
  (41 shorter events, 4.1 us)
Async XLA Ops:
  0.6 0.7 copy-start.4
  1.4 0.7 copy-start.6
  2.0 0.7 copy-start.7
  2.7 4.9 %copy-start.3 = (bf16[512,512]{1,0:T(8,128)(2,1)S(1)}, bf16[512,512]{1,0:T(8,128)(2,1)}, u32[]{:S(2)}) copy-start(bf16[512,512]{1,0:T(8,128)(2,1)} %w_own.6) | copy-start | bytes 1572868
  6.1 15.0 %copy-start = (bf16[2048,576]{0,1:T(8,128)(2,1)S(1)}, bf16[2048,576]{0,1:T(8,128)(2,1)}, u32[]{:S(2)}) copy-start(bf16[2048,576]{0,1:T(8,128)(2,1)} %param.15) | copy-start | bytes 7077892
  6.1 15.0 %copy-start.1 = (bf16[2048,384]{1,0:T(8,128)(2,1)S(1)}, bf16[2048,384]{1,0:T(8,128)(2,1)}, u32[]{:S(2)}) copy-start(bf16[2048,384]{1,0:T(8,128)(2,1)} %w_query.1) | copy-start | bytes 4718596
  6.1 15.0 %copy-start.5 = (bf16[4,2048]{1,0:T(4,128)(2,1)S(1)}, bf16[4,2048]{1,0:T(4,128)(2,1)}, u32[]{:S(2)}) copy-start(bf16[4,2048]{1,0:T(4,128)(2,1)} %x.5) | copy-start | bytes 49156
  6.1 3.3 %collective-permute-start = (bf16[1152,128]{1,0:T(8,128)(2,1)S(1)}, bf16[1152,128]{1,0:T(8,128)(2,1)S(1)}, u32[]{:S(2)}, u32[]{:S(2)}) collective-permute-start(bf16[1152,128]{1,0:T(8,128)(2,1)S(1)} %latent.1.half.refs_0_.own), channel_id=1, source_target_pairs={{0,1},{1,0},{2,3},{3,2},{4,5},{5,4},{6,7},{7,6},{8,9},{9,8},{10,11... | collective-permute-start | bytes 884744 | tf_op jit(solution)/shard_map/ppermute | solution.py:649
  7.6 24.5 %collective-permute-start.2 = (bf16[512,512]{1,0:T(8,128)(2,1)S(1)}, bf16[512,512]{1,0:T(8,128)(2,1)}, u32[]{:S(2)}, u32[]{:S(2)}) collective-permute-start(bf16[512,512]{1,0:T(8,128)(2,1)S(1)} %copy-done.3), channel_id=1, source_target_pairs={{0,1},{1,0},{2,3},{3,2},{4,5},{5,4},{6,7},{7,6},{8,9},{9,8},{10,11... | collective-permute-start | bytes 1572872 | tf_op jit(solution)/shard_map/ppermute | solution.py:649
  7.7 13.3 %collective-permute-start.3 = (bf16[1152,128]{1,0:T(8,128)(2,1)S(1)}, bf16[1152,128]{1,0:T(8,128)(2,1)S(1)}, u32[]{:S(2)}, u32[]{:S(2)}) collective-permute-start(bf16[1152,128]{1,0:T(8,128)(2,1)S(1)} %latent.1.half.refs_0_.own), channel_id=1, source_target_pairs={{0,8},{1,9},{2,26},{3,27},{4,20},{5,21},{6,38},{7,39},{8,16},{9,17... | collective-permute-start | bytes 884744 | tf_op jit(solution)/shard_map/ppermute | solution.py:643
  13.6 21.6 %copy-start.2 = (bf16[256,2048]{1,0:T(8,128)(2,1)S(1)}, bf16[256,2048]{1,0:T(8,128)(2,1)}, u32[]{:S(2)}) copy-start(bf16[256,2048]{1,0:T(8,128)(2,1)} %w_own.7) | copy-start | bytes 3145732
  13.6 25.0 %copy-start.8 = (s32[4]{0:T(128)S(1)}, s32[4]{0:T(128)}, u32[]{:S(2)}) copy-start(s32[4]{0:T(128)} %lengths.11) | copy-start | bytes 52
  13.6 24.8 %collective-permute-start.1 = (bf16[2,512,256]{2,1,0:T(8,128)(2,1)S(1)}, bf16[2,512,256]{2,1,0:T(8,128)(2,1)}, u32[]{:S(2)}, u32[]{:S(2)}) collective-permute-start(bf16[2,512,256]{2,1,0:T(8,128)(2,1)S(1)} %query.1.q_own), channel_id=1, source_target_pairs={{0,1},{1,0},{2,3},{3,2},{4,5},{5,4},{6,7},{7,6},{8,9},{9,8},{10,11... | collective-permute-start | bytes 1572872 | tf_op jit(solution)/shard_map/ppermute | solution.py:649
  21.1 14.6 %collective-permute-start.4 = (bf16[1152,128]{1,0:T(8,128)(2,1)S(1)}, bf16[1152,128]{1,0:T(8,128)(2,1)S(1)}, u32[]{:S(2)}, u32[]{:S(2)}) collective-permute-start(bf16[1152,128]{1,0:T(8,128)(2,1)S(1)} %collective-permute-done.3.refs_1_.refs_0_), channel_id=1, source_target_pairs={{0,32},{1,33},{2,34},{3,35},{4,36},{5,37},{6,38},{7,39},{8,40},{9,... | collective-permute-start | bytes 884744 | tf_op jit(solution)/shard_map/ppermute | solution.py:643
  24.5 10.7 %all-to-all-start = ((f32[16,8,256]{2,1,0:T(8,128)}), f32[16,8,256]{2,1,0:T(8,128)S(1)}, u32[]{:S(2)}, u32[]{:S(2)}) async-start(f32[16,8,256]{2,1,0:T(8,128)} %bitcast.2), calls=%async_computation | async-start | bytes 262144 | tf_op jit(solution)/shard_map/all_to_all | solution.py:674
  28.5 14.1 %collective-permute-start.10 = (bf16[1152,128]{1,0:T(8,128)(2,1)S(1)}, bf16[1152,128]{1,0:T(8,128)(2,1)S(1)}, u32[]{:S(2)}, u32[]{:S(2)}) collective-permute-start(bf16[1152,128]{1,0:T(8,128)(2,1)S(1)} %collective-permute-done.3.refs_1_.refs_0_), channel_id=1, source_target_pairs={{0,6},{1,7},{2,0},{3,1},{4,2},{5,3},{6,4},{7,5},{8,14},{9,15},{10,... | collective-permute-start | bytes 884744 | tf_op jit(solution)/shard_map/ppermute | solution.py:646
  30.8 14.7 %collective-permute-start.8 = (bf16[1152,128]{1,0:T(8,128)(2,1)S(1)}, bf16[1152,128]{1,0:T(8,128)(2,1)}, u32[]{:S(2)}, u32[]{:S(2)}) collective-permute-start(bf16[1152,128]{1,0:T(8,128)(2,1)S(1)} %collective-permute-done.3.refs_1_.refs_0_), channel_id=1, source_target_pairs={{0,8},{1,9},{2,10},{3,11},{4,124},{5,125},{6,126},{7,127},{8,16},{... | collective-permute-start | bytes 884744 | tf_op jit(solution)/shard_map/ppermute | solution.py:643
  32.1 14.5 %collective-permute-start.9 = (bf16[1152,128]{1,0:T(8,128)(2,1)S(1)}, bf16[1152,128]{1,0:T(8,128)(2,1)}, u32[]{:S(2)}, u32[]{:S(2)}) collective-permute-start(bf16[1152,128]{1,0:T(8,128)(2,1)S(1)} %collective-permute-done.3.refs_1_.refs_0_), channel_id=1, source_target_pairs={{0,2},{1,3},{2,4},{3,5},{4,6},{5,7},{6,0},{7,1},{8,10},{9,11},{10,... | collective-permute-start | bytes 884744 | tf_op jit(solution)/shard_map/ppermute | solution.py:646
  35.6 29.0 %collective-permute-start.12 = (bf16[256,2048]{1,0:T(8,128)(2,1)S(1)}, bf16[256,2048]{1,0:T(8,128)(2,1)S(1)}, u32[]{:S(2)}, u32[]{:S(2)}) collective-permute-start(bf16[256,2048]{1,0:T(8,128)(2,1)S(1)} %copy-done.2), channel_id=1, source_target_pairs={{0,1},{1,0},{2,3},{3,2},{4,5},{5,4},{6,7},{7,6},{8,9},{9,8},{10,11... | collective-permute-start | bytes 3145736 | tf_op jit(solution)/shard_map/ppermute | solution.py:649
  38.5 14.6 %collective-permute-start.5 = (bf16[1152,128]{1,0:T(8,128)(2,1)S(1)}, bf16[1152,128]{1,0:T(8,128)(2,1)S(1)}, u32[]{:S(2)}, u32[]{:S(2)}) collective-permute-start(bf16[1152,128]{1,0:T(8,128)(2,1)S(1)} %collective-permute-done.4.refs_3_.refs_4_), channel_id=1, source_target_pairs={{0,8},{1,9},{2,10},{3,11},{4,124},{5,125},{6,126},{7,127},{8,16},{... | collective-permute-start | bytes 884744 | tf_op jit(solution)/shard_map/ppermute | solution.py:643
  42.6 10.8 %collective-permute-start.6 = (bf16[1152,128]{1,0:T(8,128)(2,1)S(1)}, bf16[1152,128]{1,0:T(8,128)(2,1)S(1)}, u32[]{:S(2)}, u32[]{:S(2)}) collective-permute-start(bf16[1152,128]{1,0:T(8,128)(2,1)S(1)} %collective-permute-done.4.refs_3_.refs_4_), channel_id=1, source_target_pairs={{0,2},{1,3},{2,4},{3,5},{4,6},{5,7},{6,0},{7,1},{8,10},{9,11},{10,... | collective-permute-start | bytes 884744 | tf_op jit(solution)/shard_map/ppermute | solution.py:646
  45.5 9.0 %collective-permute-start.7 = (bf16[1152,128]{1,0:T(8,128)(2,1)S(1)}, bf16[1152,128]{1,0:T(8,128)(2,1)S(1)}, u32[]{:S(2)}, u32[]{:S(2)}) collective-permute-start(bf16[1152,128]{1,0:T(8,128)(2,1)S(1)} %collective-permute-done.4.refs_3_.refs_4_), channel_id=1, source_target_pairs={{0,6},{1,7},{2,0},{3,1},{4,2},{5,3},{6,4},{7,5},{8,14},{9,15},{10,... | collective-permute-start | bytes 884744 | tf_op jit(solution)/shard_map/ppermute | solution.py:646
  53.0 8.9 %copy-start.9 = (s32[64]{0:T(128)S(1)}, s32[64]{0:T(128)}, u32[]{:S(2)}) copy-start(s32[64]{0:T(128)} %table.3) | copy-start | bytes 772
  60.6 3.9 %collective-permute-start.11 = (f32[256,640]{1,0:T(8,128)S(1)}, f32[256,640]{1,0:T(8,128)S(1)}, u32[]{:S(2)}, u32[]{:S(2)}) collective-permute-start(f32[256,640]{1,0:T(8,128)S(1)} %get-tuple-element.18), channel_id=1, source_target_pairs={{0,1},{1,0},{2,3},{3,2},{4,5},{5,4},{6,7},{7,6},{8,9},{9,8},{10,11... | collective-permute-start | bytes 1966088 | tf_op jit(solution)/shard_map/ppermute | solution.py:649
  63.2 10.9 %collective-permute-start.16 = (bf16[1280,128]{1,0:T(8,128)(2,1)S(1)}, bf16[1280,128]{1,0:T(8,128)(2,1)S(1)}, u32[]{:S(2)}, u32[]{:S(2)}) collective-permute-start(bf16[1280,128]{1,0:T(8,128)(2,1)S(1)} %get-tuple-element.25), channel_id=1, source_target_pairs={{0,64},{1,65},{2,66},{3,67},{4,68},{5,69},{6,70},{7,71},{8,72},{9,... | collective-permute-start | bytes 983048 | tf_op jit(solution)/shard_map/ppermute | solution.py:643
  66.2 9.6 %collective-permute-start.13 = (bf16[72,2048]{1,0:T(8,128)(2,1)S(1)}, bf16[72,2048]{1,0:T(8,128)(2,1)S(1)}, u32[]{:S(2)}, u32[]{:S(2)}) collective-permute-start(bf16[72,2048]{1,0:T(8,128)(2,1)S(1)} %get-tuple-element.21), channel_id=1, source_target_pairs={{0,2},{1,3},{2,4},{3,5},{4,6},{5,7},{6,0},{7,1},{8,10},{9,11},{10,... | collective-permute-start | bytes 884744 | tf_op jit(solution)/shard_map/ppermute | solution.py:646
  67.7 14.3 %collective-permute-start.14 = (bf16[72,2048]{1,0:T(8,128)(2,1)S(1)}, bf16[72,2048]{1,0:T(8,128)(2,1)S(1)}, u32[]{:S(2)}, u32[]{:S(2)}) collective-permute-start(bf16[72,2048]{1,0:T(8,128)(2,1)S(1)} %get-tuple-element.22), channel_id=1, source_target_pairs={{0,4},{1,5},{2,6},{3,7},{4,0},{5,1},{6,2},{7,3},{8,12},{9,13},{10,... | collective-permute-start | bytes 884744 | tf_op jit(solution)/shard_map/ppermute | solution.py:646
  68.8 13.5 %collective-permute-start.15 = (bf16[72,2048]{1,0:T(8,128)(2,1)S(1)}, bf16[72,2048]{1,0:T(8,128)(2,1)S(1)}, u32[]{:S(2)}, u32[]{:S(2)}) collective-permute-start(bf16[72,2048]{1,0:T(8,128)(2,1)S(1)} %get-tuple-element.23), channel_id=1, source_target_pairs={{0,6},{1,7},{2,0},{3,1},{4,2},{5,3},{6,4},{7,5},{8,14},{9,15},{10,... | collective-permute-start | bytes 884744 | tf_op jit(solution)/shard_map/ppermute | solution.py:646
  74.7 9.9 %collective-permute-start.17 = (bf16[1280,128]{1,0:T(8,128)(2,1)S(1)}, bf16[1280,128]{1,0:T(8,128)(2,1)S(1)}, u32[]{:S(2)}, u32[]{:S(2)}) collective-permute-start(bf16[1280,128]{1,0:T(8,128)(2,1)S(1)} %choose.1.own), channel_id=1, source_target_pairs={{0,1},{1,0},{2,3},{3,2},{4,5},{5,4},{6,7},{7,6},{8,9},{9,8},{10,11... | collective-permute-start | bytes 983048 | tf_op jit(solution)/shard_map/ppermute | solution.py:649
  83.2 2.5 %collective-permute-start.18 = (f32[8,2048]{1,0:T(8,128)S(1)}, f32[8,2048]{1,0:T(8,128)S(1)}, u32[]{:S(2)}, u32[]{:S(2)}) collective-permute-start(f32[8,2048]{1,0:T(8,128)S(1)} %get-tuple-element.26), channel_id=1, source_target_pairs={{0,1},{1,0},{2,3},{3,2},{4,5},{5,4},{6,7},{7,6},{8,9},{9,8},{10,11... | collective-permute-start | bytes 196616 | tf_op jit(solution)/shard_map/ppermute | solution.py:649

commit v2 on v1

--- a/solution.py
+++ b/solution.py
@@ -23,7 +23,8 @@
 FREQ = (
     ROPE_BASE ** (-(np.arange(ROPE // 2, dtype=np.float64) * 2.0 / ROPE))
 ).astype(np.float32)[:, None]
-ATTEND_MIB = {"first": 14, "middle": 16, "last": 16}
+ATTEND_MIB = {"first": 16, "last": 24}
+COST = {"first": 1 << 20, "last": 8 << 30}
 EXTRA = 8
 
 F32 = jnp.float32
@@ -66,6 +67,11 @@
 
 def tokens_of(ref):
     return ref.shape[0] * 128 // (RANK + ROPE)
+
+
+def halves_of(pairs):
+    n = pairs[0].shape[0] // 2
+    return [p.at[pl.ds(i * n, n)] for p in pairs for i in range(2)]
 
 
 def latent_rows(ref):
@@ -160,11 +166,64 @@
         out_specs=pl.BlockSpec((n * width // 128, 128), lambda i: (0, 0)),
         out_shape=jax.ShapeDtypeStruct((n * width // 128, 128), BF16),
         scratch_shapes=[pltpu.VMEM((n, 2 * ROPE), F32), pltpu.VMEM((n, width), F32)],
-        compiler_params=params(14),
+        compiler_params=params(60),
         cost_estimate=pl.CostEstimate(
             flops=2 * n * d * width, bytes_accessed=4 << 20, transcendentals=0
         ),
     )(lengths, in_hbm(x), in_hbm(w_down_t), gain, FREQ)
+
+
+def after_kernel(x, _, out):
+    pass
+
+
+def passed(x, after):
+    return pl.pallas_call(
+        after_kernel,
+        name="passed",
+        in_specs=[anywhere()] * 2,
+        out_specs=anywhere(),
+        out_shape=jax.ShapeDtypeStruct(x.shape, x.dtype),
+        input_output_aliases={0: 0},
+        compiler_params=params(4),
+    )(x, after)
+
+
+def first_part_kernel(x, out, sem):
+    copy = pltpu.make_async_copy(x, out.at[pl.ds(0, x.shape[0])], sem)
+    copy.start()
+    copy.wait()
+
+
+def second_part_kernel(x, _, out, sem):
+    copy = pltpu.make_async_copy(x, out.at[pl.ds(x.shape[0], x.shape[0])], sem)
+    copy.start()
+    copy.wait()
+
+
+def first_part(x):
+    return pl.pallas_call(
+        first_part_kernel,
+        name="first_part",
+        in_specs=[anywhere()],
+        out_specs=anywhere(),
+        out_shape=jax.ShapeDtypeStruct((2 * x.shape[0], x.shape[1]), x.dtype),
+        scratch_shapes=[pltpu.SemaphoreType.DMA],
+        compiler_params=params(4),
+    )(x)
+
+
+def second_part(x, both):
+    return pl.pallas_call(
+        second_part_kernel,
+        name="second_part",
+        in_specs=[anywhere()] * 2,
+        out_specs=anywhere(),
+        out_shape=jax.ShapeDtypeStruct(both.shape, both.dtype),
+        scratch_shapes=[pltpu.SemaphoreType.DMA],
+        input_output_aliases={1: 0},
+        compiler_params=params(4),
+    )(x, both)
 
 
 def query_kernel(lengths, x, w, freq, _, out, cs, acc):
@@ -317,14 +376,12 @@
 
 
 def attend_kernel(stage, places, lengths, q_own, q_sib, w_own, w_sib, *refs):
-    nseg = len(places)
-    segs, refs = refs[:nseg], refs[nseg:]
+    segs, refs = refs[:3], refs[3:]
     if stage == "first":
         _, acc_out, rbuf, kbuf, vbuf, sbuf = refs
-    elif stage == "middle":
-        acc_in, _, acc_out, rbuf, kbuf, vbuf, sbuf = refs
     else:
         acc_in, _, mine, other, rbuf, kbuf, vbuf, sbuf, tile = refs
+        segs = halves_of(segs)
     tok = q_own.shape[1]
     heads = 4
     ctx, chip, core = place_of()
@@ -451,14 +508,14 @@
         scratch_shapes=scratch,
         compiler_params=params(ATTEND_MIB[stage]),
         cost_estimate=pl.CostEstimate(
-            flops=2 * heads * tok * keys * 1024,
-            bytes_accessed=8 << 20,
-            transcendentals=heads * tok * keys,
+            flops=COST[stage],
+            bytes_accessed=1 << 16,
+            transcendentals=0,
         ),
     )(*args)
 
 
-def merge_kernel(mine, came, w_own, w_sib, dec, _, out0, out1, out2, out3, heads):
+def merge_kernel(mine, came, w_own, w_sib, dec, dec_sib, _, out0, out1, out2, out3, heads):
     _, chip, _ = place_of()
     wide = 4 * VDIM
     for h in range(4):
@@ -481,20 +538,32 @@
     )
     got = jnp.dot(part[:, : 2 * VDIM], w_own[...], preferred_element_type=F32)
     got = got + jnp.dot(part[:, 2 * VDIM :], w_sib[...], preferred_element_type=F32)
-    for i, out in enumerate((out0, out1, out2, out3)):
-        out[:quarter, :] = got[i * quarter : (i + 1) * quarter].astype(out.dtype)
-        out[quarter:, :] = dec[...].astype(out.dtype)
-
-
-def merge_out(mine, came, w_own, w_sib, dec, after):
+    both = dec[...]
+    wide = both.shape[1] // 2
+    packed = jnp.concatenate(
+        [
+            jnp.concatenate([both[:4, g : g + 128], both[:4, wide + g : wide + g + 128]], 0)
+            for g in range(0, wide, 128)
+        ],
+        0,
+    )
+    parts = [
+        jnp.concatenate([got[i * quarter : (i + 1) * quarter], packed], 1) for i in range(4)
+    ]
+    out0[...] = parts[0]
+    out1[...] = parts[1].astype(BF16)
+    out2[...] = parts[2].astype(BF16)
+    out3[...] = parts[3].astype(BF16)
+
+
+def merge_out(mine, came, w_own, w_sib, dec, dec_sib, after):
     rows, d = mine.shape[0], w_own.shape[1]
-    shapes = [
-        jax.ShapeDtypeStruct((rows // 4 + EXTRA, d), F32 if i == 0 else BF16) for i in range(4)
-    ]
+    shapes = [jax.ShapeDtypeStruct((rows // 4, d + 128), F32)]
+    shapes += [jax.ShapeDtypeStruct((rows // 4, d + 128), BF16)] * 3
     return pl.pallas_call(
         merge_kernel,
         name="merge_out",
-        in_specs=[whole()] * 5 + [anywhere()],
+        in_specs=[whole()] * 6 + [anywhere()],
         out_specs=[whole()] * 4,
         out_shape=shapes,
         scratch_shapes=[pltpu.VMEM((rows, 4 * VDIM), BF16)],
@@ -502,26 +571,30 @@
         cost_estimate=pl.CostEstimate(
             flops=2 * rows * 512 * d, bytes_accessed=5 << 20, transcendentals=0
         ),
-    )(mine, came, w_own, w_sib, dec, after)
+    )(mine, came, w_own, w_sib, dec, dec_sib, after)
 
 
 def sum_kernel(own, a, b, c, out, dec):
     rows = out.shape[0]
     got = own[...] + a[...].astype(F32) + b[...].astype(F32) + c[...].astype(F32)
-    out[...] = got[:rows].astype(BF16)
-    dec[...] = got[rows:]
-
-
-def sum_parts(own, a, b, c):
-    rows, d = own.shape
+    d = out.shape[1]
+    out[...] = got[:, :d].astype(BF16)
+    for i in range(rows // 8):
+        piece = got[8 * i : 8 * i + 8, d:]
+        dec[:, 128 * i : 128 * i + 128] = piece[:4]
+        dec[:, d // 2 + 128 * i : d // 2 + 128 * i + 128] = piece[4:]
+
+
+def sum_parts(own, a, b, c, requests):
+    rows, d = own.shape[0], own.shape[1] - 128
     return pl.pallas_call(
         sum_kernel,
         name="sum_parts",
         in_specs=[whole()] * 4,
         out_specs=[whole()] * 2,
         out_shape=[
-            jax.ShapeDtypeStruct((rows - EXTRA, d), BF16),
-            jax.ShapeDtypeStruct((EXTRA, d), F32),
+            jax.ShapeDtypeStruct((rows, d), BF16),
+            jax.ShapeDtypeStruct((requests, d), F32),
         ],
         compiler_params=params(16),
         cost_estimate=pl.CostEstimate(
@@ -539,11 +612,11 @@
 
 
 def pages_kernel(table, own, *refs):
-    halves, (_, near, far) = refs[:8], refs[8:]
+    near0, far0, *pairs, _, near, far = refs
     _, chip, core = place_of()
     held = [(own, 0)]
-    for i, half in enumerate(halves):
-        held.append((half, back_of(chip + i % 4) + i // 4 * 4))
+    for i, half in enumerate([near0, far0] + halves_of(pairs)):
+        held.append((half, back_of(chip + i // 2) + i % 2 * 4))
 
     def copy(half, i, out):
         n = tokens_of(half)
@@ -572,7 +645,7 @@
     return pl.pallas_call(
         pages_kernel,
         name="pages",
-        in_specs=[smem()] + [whole()] * 9 + [anywhere()],
+        in_specs=[smem()] + [whole()] * 6 + [anywhere()],
         out_specs=[whole()] * 2,
         out_shape=[jax.ShapeDtypeStruct((PAGES_DEV // 2 * SLOT, 128), BF16)] * 2,
         compiler_params=params(16),
@@ -626,7 +699,7 @@
         out_specs=whole(),
         out_shape=jax.ShapeDtypeStruct((RANK + ROPE, tok), BF16),
         compiler_params=params(16),
-    )(own, came).T
+    )(own, came)
 
 
 def on_device(
@@ -658,48 +731,48 @@
     half = latent_of(lengths, prompt_states, w_down_t, gain)
     near0 = over_ctx(half, chip_dist)
     half_sib = to_sibling(half)
-    q_own = query_of(lengths, prompt_states, w_query, half_sib)
-    q_sib = to_sibling(q_own)
-    far0 = over_ctx(near0, lambda j: 4)
-    near2 = over_ctx(near0, lambda j: chip_dist(j, 2) - chip_dist(j))
-    near3 = over_x(near0, 1)
-    near1 = over_x(near0, -1)
-    far2 = over_ctx(far0, lambda j: chip_dist(j, 2) - chip_dist(j))
-    far3 = over_x(far0, 1)
-    far1 = over_x(far0, -1)
 
     dpart, dself = decode_partial(
         n_ctx, lengths, decode_states, w_query, w_down_t, gain, w_up, half, half_sib
     )
     parts = lax.all_to_all(dpart, "ctx", 0, 0, tiled=True)
 
+    q_own = query_of(lengths, prompt_states, w_query, parts)
+    q_sib = to_sibling(q_own)
+    near0 = passed(near0, dpart)
+    far0 = over_ctx(near0, lambda j: 4)
+    pair0 = second_part(far0, first_part(near0))
+    pair3 = over_x(pair0, 1)
+    pair1 = over_x(pair0, -1)
+    pair2 = over_ctx(pair0, lambda j: chip_dist(j, 2) - chip_dist(j))
+
     weights = (q_own, q_sib, w_up, w_up_sib)
-    state = attend("first", lengths, *weights, [half, near0], (None, (0, 0)), [dpart])
+    state = attend(
+        "first", lengths, *weights, [half, near0, far0], (None, (0, 0), (0, 4)), [dself]
+    )
     dec = decode_merge(parts, dself, w_out, dself)
-    state = attend(
-        "middle",
+    mine, other = attend(
+        "last",
         lengths,
         *weights,
-        [near2, near3, near1, far0],
-        ((2, 0), (3, 0), (1, 0), (0, 4)),
-        (*state, dpart),
-    )
-    mine, other = attend(
-        "last", lengths, *weights, [far2, far3, far1], ((2, 4), (3, 4), (1, 4)), (*state, dec)
+        [pair1, pair2, pair3],
+        ((1, 0), (1, 4), (2, 0), (2, 4), (3, 0), (3, 4)),
+        (*state, dec),
     )
     came = to_sibling(other)
-    halves = [near0, near1, near2, near3, far0, far1, far2, far3]
-    page_near, page_far = pages_of(page_table, half, halves, mine)
-    out0, out1, out2, out3 = merge_out(mine, came, w_out, w_out_sib, dec, page_near)
+    page_near, page_far = pages_of(page_table, half, [near0, far0, pair1, pair2, pair3], mine)
+    out0, out1, out2, out3 = merge_out(mine, came, w_out, w_out_sib, dec, dec, page_near)
+    got2 = over_x(out2, 2)
     got1 = over_x(out1, 1)
     got3 = over_x(out3, -1)
-    got2 = over_x(out2, 2)
-    prefill_out, dec = sum_parts(out0, got1, got2, got3)
-    decode_out = (dec + to_sibling(dec))[: decode_states.shape[0]].astype(BF16)
 
     page = choose(page_table, page_near, over_ctx(page_far, lambda j: 8))
-    paged_cache = cache_of(page, to_sibling(page), prompt_states.shape[0])
-    return (prefill_out, paged_cache, decode_out)
+    cache_t = cache_of(page, to_sibling(page), prompt_states.shape[0])
+    prefill_out, decode_out = sum_parts(
+        out0, got1, got2, got3, decode_states.shape[0]
+    )
+    decode_out = (decode_out + to_sibling(decode_out)).astype(BF16)
+    return (prefill_out, cache_t.T, decode_out)
 
 
 def solution(mesh):

time: 86.7 us -> 80.7 us (0.931)
  starting transfers between devices: 27.8 us -> 22.3 us
  Pallas kernels: 33.2 us -> 31.6 us
  waiting for transfers between devices: 21.8 us -> 22.8 us
    ppermute x5 -> x4, waiting for transfers between devices: 10.4 us -> 17.1 us  [over_ctx(): return lax.ppermute(block, ('ctx', 'head'), route)]
    ppermute x7 -> x5, starting transfers between devices: 10.4 us -> 5.37 us  [over_x(): lax.ppermute(block, 'head', [(j, (j + 2 * s) % n_head) for j in range(n_h...]
    pallas_call x3 -> x2, Pallas kernels: 16.6 us -> 13 us  [attend(): pl.pallas_call(functools.partial(attend_kernel, stage, places), name='att...]
    ppermute x7 -> x5, waiting for transfers between devices: 8.22 us -> 4.91 us  [over_x(): lax.ppermute(block, 'head', [(j, (j + 2 * s) % n_head) for j in range(n_h...]
    all_to_all x1, waiting for transfers between devices: 3.1 us -> 0.01 us  [on_device(): parts = lax.all_to_all(dpart, 'ctx', 0, 0, tiled=True)]
    ppermute x5 -> x4, starting transfers between devices: 4.53 us -> 2.2 us  [over_ctx(): return lax.ppermute(block, ('ctx', 'head'), route)]
    ppermute x7, starting transfers between devices: 8.81 us -> 10.7 us  [to_sibling(): return lax.ppermute(block, 'head', [(j, j ^ 1) for j in range(n_head)])]
    pallas_call x1 -> x4, Pallas kernels: 1.56 us -> 2.63 us  [the longest x1 1.59 us: merge_out(): pl.pallas_call(merge_kernel, name='merge_out', in_specs=[whole()] * 6 + [...]
  transfers between devices with their start and end apart: 20 -> 17, of which waited for: 8 -> 8; matrix products, arithmetic and copies ran while one was open for 0% -> 0% of each run, Pallas kernels for 35% -> 34%
where the time goes in v2:
time: 80.7 us; the launch traced here: 80.3 us
  Pallas kernels  31.6 us (39%)
  waiting for transfers between devices  22.8 us (28%)
  starting transfers between devices  22.3 us (28%)
  local copies, waits for them, and re-layouts  2.06 us (3%)
  between operations  0.83 us (1%)
    ppermute x4, waiting for transfers between devices, over_ctx(): return lax.ppermute(block, ('ctx', 'head'), route)  17.1 us
    pallas_call x2, Pallas kernels, attend(): pl.pallas_call(functools.partial(attend_kernel, stage, places), name='att...  13 us
    ppermute x7, starting transfers between devices, to_sibling(): return lax.ppermute(block, 'head', [(j, j ^ 1) for j in range(n_head)])  10.7 us
    ppermute x5, starting transfers between devices, over_x(): lax.ppermute(block, 'head', [(j, (j + 2 * s) % n_head) for j in range(n_h...  5.37 us
    ppermute x5, waiting for transfers between devices, over_x(): lax.ppermute(block, 'head', [(j, (j + 2 * s) % n_head) for j in range(n_h...  4.91 us
    pallas_call x1, Pallas kernels, query_of(): pl.pallas_call(query_kernel, name='query', grid=(steps,), in_specs=[smem(...  4.27 us
    pallas_call x1, Pallas kernels, latent_of(): pl.pallas_call(latent_kernel, name='latent', grid=(steps,), in_specs=[sme...  4.2 us
    all_to_all x1, starting transfers between devices, on_device(): parts = lax.all_to_all(dpart, 'ctx', 0, 0, tiled=True)  4.05 us
  transfers between devices with their start and end apart: 17, of which 8 were waited for; matrix products, arithmetic and copies ran while one was open for 0% of the time, Pallas kernels for 34%

profile of v2, /device:TPU:1, one launch (start us, length us, event | category | flops | bytes accessed | tf_op | source)
XLA Modules:
  0.0 80.3 jit_solution(1444309487992908799)
XLA Ops:
  0.7 4.2 %latent.1.half.refs_0_.own = bf16[1152,128]{1,0:T(8,128)(2,1)} custom-call(s32[4]{0:T(128)} %lengths.9, bf16[512,2048]{1,0:T(8,128)(2,1)} %x.5, bf16[576,2048]{1,0:T(8,128)(2,1)} %bitcast.5, f32[1,512]{1,0:T(1,128)} %bitcast.9, f32[32,1]{1,0:T(8,128)} %constant.2.clone.freq), custom_call_target="tpu_custom_call" | custom-call | flops 603979776 | bytes 4194304 | tf_op jit(solution)/shard_map/latent/pallas_call | solution.py:155
  4.9 1.4 %collective-permute-start = (bf16[1152,128]{1,0:T(8,128)(2,1)}, bf16[1152,128]{1,0:T(8,128)(2,1)S(1)}, u32[]{:S(2)}, u32[]{:S(2)}) collective-permute-start(bf16[1152,128]{1,0:T(8,128)(2,1)} %latent.1.half.refs_0_.own), channel_id=1, source_target_pairs={{0,1},{1,0},{2,3},{3,2},{4,5},{5,4},{6,7},{7,6},{8,9},{9,8},{10,11... | collective-permute-start | bytes 884744 | tf_op jit(solution)/shard_map/ppermute | solution.py:722
  6.3 1.7 %collective-permute-start.3 = (bf16[1152,128]{1,0:T(8,128)(2,1)}, bf16[1152,128]{1,0:T(8,128)(2,1)}, u32[]{:S(2)}, u32[]{:S(2)}) collective-permute-start(bf16[1152,128]{1,0:T(8,128)(2,1)} %latent.1.half.refs_0_.own), channel_id=1, source_target_pairs={{0,8},{1,9},{2,26},{3,27},{4,20},{5,21},{6,38},{7,39},{8,16},{9,17... | collective-permute-start | bytes 884744 | tf_op jit(solution)/shard_map/ppermute | solution.py:716
  8.1 1.0 %copy-done.2 = bf16[1152,128]{1,0:T(8,128)(2,1)S(1)} copy-done((bf16[1152,128]{1,0:T(8,128)(2,1)S(1)}, bf16[1152,128]{1,0:T(8,128)(2,1)}, u32[]{:S(2)}) %copy-start.2) | copy-done | bytes 294936
  9.1 1.0 %copy-done.5 = bf16[512,512]{1,0:T(8,128)(2,1)S(1)} copy-done((bf16[512,512]{1,0:T(8,128)(2,1)S(1)}, bf16[512,512]{1,0:T(8,128)(2,1)}, u32[]{:S(2)}) %copy-start.5) | copy-done | bytes 524312
  10.1 3.4 %decode_partial.1 = (f32[128,256]{1,0:T(8,128)}, f32[8,256]{1,0:T(8,128)S(1)}) custom-call(s32[4]{0:T(128)S(1)} %copy-done.10, bf16[4,2048]{1,0:T(4,128)(2,1)S(1)} %copy-done.8, bf16[2048,384]{1,0:T(8,128)(2,1)S(1)} %copy-done.1, bf16[576,2048]{1,0:T(8,128)(2,1)S(1)} %bitcast.6, f32[1,512]{1,0:T(1,128)S(1)} %bitcast.10, f32[32,1]{1,0:T(8,128)S(1)} %copy-done.7, ...), custom_call_target="tpu_custom_call" | custom-call | flops 1048576 | bytes 65536 | tf_op jit(solution)/shard_map/decode_partial/pallas_call | solution.py:333
  13.5 6.8 %collective-permute-done.3.x = bf16[1152,128]{1,0:T(8,128)(2,1)} collective-permute-done((bf16[1152,128]{1,0:T(8,128)(2,1)}, bf16[1152,128]{1,0:T(8,128)(2,1)}, u32[]{:S(2)}, u32[]{:S(2)}) %collective-permute-start.3) | collective-permute-done | bytes 294944 | tf_op jit(solution)/shard_map/ppermute | solution.py:716
  20.3 4.1 %all-to-all-start = ((f32[16,8,256]{2,1,0:T(8,128)}), f32[16,8,256]{2,1,0:T(8,128)S(1)}, u32[]{:S(2)}, u32[]{:S(2)}) async-start(f32[16,8,256]{2,1,0:T(8,128)} %bitcast.2), calls=%async_computation | async-start | bytes 262144 | tf_op jit(solution)/shard_map/all_to_all | solution.py:738
  24.4 1.0 %first_part.1._ = bf16[2304,128]{1,0:T(8,128)(2,1)S(1)} custom-call(bf16[1152,128]{1,0:T(8,128)(2,1)} %passed.1.x.refs_1_.refs_0_), custom_call_target="tpu_custom_call" | custom-call | tf_op jit(solution)/shard_map/first_part/pallas_call | solution.py:205
  25.4 4.6 %collective-permute-done.4.x.refs_2_.refs_1_ = bf16[1152,128]{1,0:T(8,128)(2,1)S(1)} collective-permute-done((bf16[1152,128]{1,0:T(8,128)(2,1)}, bf16[1152,128]{1,0:T(8,128)(2,1)S(1)}, u32[]{:S(2)}, u32[]{:S(2)}) %collective-permute-start.4) | collective-permute-done | bytes 294944 | tf_op jit(solution)/shard_map/ppermute | solution.py:716
  30.2 1.4 %collective-permute-start.7 = (bf16[2304,128]{1,0:T(8,128)(2,1)S(1)}, bf16[2304,128]{1,0:T(8,128)(2,1)S(1)}, u32[]{:S(2)}, u32[]{:S(2)}) collective-permute-start(bf16[2304,128]{1,0:T(8,128)(2,1)S(1)} %second_part.1), channel_id=1, source_target_pairs={{0,2},{1,3},{2,4},{3,5},{4,6},{5,7},{6,0},{7,1},{8,10},{9,11},{10,... | collective-permute-start | bytes 1769480 | tf_op jit(solution)/shard_map/ppermute | solution.py:719
  31.6 2.8 %collective-permute-start.2 = (bf16[512,512]{1,0:T(8,128)(2,1)S(1)}, bf16[512,512]{1,0:T(8,128)(2,1)}, u32[]{:S(2)}, u32[]{:S(2)}) collective-permute-start(bf16[512,512]{1,0:T(8,128)(2,1)S(1)} %copy-done.6), channel_id=1, source_target_pairs={{0,1},{1,0},{2,3},{3,2},{4,5},{5,4},{6,7},{7,6},{8,9},{9,8},{10,11... | collective-permute-start | bytes 1572872 | tf_op jit(solution)/shard_map/ppermute | solution.py:722
  34.4 4.3 %query.1.q_own = bf16[2,512,256]{2,1,0:T(8,128)(2,1)S(1)} custom-call(s32[4]{0:T(128)S(1)} %copy-done.10, bf16[512,2048]{1,0:T(8,128)(2,1)} %x.5, bf16[2048,384]{1,0:T(8,128)(2,1)} %w.1, f32[32,1]{1,0:T(8,128)S(1)} %copy-done.7, f32[128,256]{1,0:T(8,128)S(1)} %bitcast.7), custom_call_target="tpu_custom_call" | custom-call | flops 1048576 | bytes 65536 | tf_op jit(solution)/shard_map/query/pallas_call | solution.py:261
  39.2 0.7 collective-permute-start.9
  39.9 0.8 collective-permute-done.1.q_sib
  40.7 4.8 %attend_first.1.refs_3_ = f32[4,512,256]{2,1,0:T(8,128)S(1)} custom-call(s32[4]{0:T(128)S(1)} %copy-done.10, bf16[2,512,256]{2,1,0:T(8,128)(2,1)S(1)} %query.1.q_own, bf16[2,512,256]{2,1,0:T(8,128)(2,1)S(1)} %collective-permute-done.1.q_sib, bf16[512,512]{1,0:T(8,128)(2,1)S(1)} %copy-done.6, bf16[512,512]{1,0:T(8,128)(2,1)} %collective-permute-done.2.w_sib, ...), custom_call_target="tpu_custom_call" | custom-call | flops 1048576 | bytes 65536 | tf_op jit(solution)/shard_map/attend_first/pallas_call | solution.py:502
  45.5 0.6 collective-permute-done.6.refs_1_.refs_3_
  46.1 8.2 %attend_last.1 = (f32[256,640]{1,0:T(8,128)S(1)}, f32[256,640]{1,0:T(8,128)S(1)}) custom-call(s32[4]{0:T(128)S(1)} %copy-done.10, bf16[2,512,256]{2,1,0:T(8,128)(2,1)S(1)} %query.1.q_own, bf16[2,512,256]{2,1,0:T(8,128)(2,1)S(1)} %collective-permute-done.1.q_sib, bf16[512,512]{1,0:T(8,128)(2,1)S(1)} %copy-done.6, ...), custom_call_target="tpu_custom_call" | custom-call | flops 8589934592 | bytes 65536 | tf_op jit(solution)/shard_map/attend_last/pallas_call | solution.py:502
  54.3 3.2 %collective-permute-start.8 = (f32[256,640]{1,0:T(8,128)S(1)}, f32[256,640]{1,0:T(8,128)S(1)}, u32[]{:S(2)}, u32[]{:S(2)}) collective-permute-start(f32[256,640]{1,0:T(8,128)S(1)} %get-tuple-element.18), channel_id=1, source_target_pairs={{0,1},{1,0},{2,3},{3,2},{4,5},{5,4},{6,7},{7,6},{8,9},{9,8},{10,11... | collective-permute-start | bytes 1966088 | tf_op jit(solution)/shard_map/ppermute | solution.py:722
  57.5 1.3 %pages.1 = (bf16[1280,128]{1,0:T(8,128)(2,1)S(1)}, bf16[1280,128]{1,0:T(8,128)(2,1)S(1)}) custom-call(s32[64]{0:T(128)S(1)} %copy-done.11, bf16[1152,128]{1,0:T(8,128)(2,1)S(1)} %copy-done.3, bf16[1152,128]{1,0:T(8,128)(2,1)} %passed.1.x.refs_1_.refs_0_, bf16[1152,128]{1,0:T(8,128)(2,1)S(1)} %collective-permute-done.4.x.refs_2_.refs_1_, ...), custom_call_target="tpu_custom_call" | custom-call | tf_op jit(solution)/shard_map/pages/pallas_call | solution.py:645
  59.3 1.6 %merge_out.1 = (f32[64,2176]{1,0:T(8,128)S(1)}, bf16[64,2176]{1,0:T(8,128)(2,1)S(1)}, bf16[64,2176]{1,0:T(8,128)(2,1)S(1)}, bf16[64,2176]{1,0:T(8,128)(2,1)S(1)}) custom-call(f32[256,640]{1,0:T(8,128)S(1)} %get-tuple-element.17.refs_5_.mine, f32[256,640]{1,0:T(8,128)S(1)} %collective-permute-done.8.came, bf16[256,2048]{1,0:T(8,128)(2,1)S(1)} %copy-done.4, ...), custom_call_target="tpu_custom_call" | custom-call | flops 536870912 | bytes 5242880 | tf_op jit(solution)/shard_map/merge_out/pallas_call | solution.py:563
  60.9 1.5 %collective-permute-start.10 = (bf16[64,2176]{1,0:T(8,128)(2,1)S(1)}, bf16[64,2176]{1,0:T(8,128)(2,1)S(1)}, u32[]{:S(2)}, u32[]{:S(2)}) collective-permute-start(bf16[64,2176]{1,0:T(8,128)(2,1)S(1)} %get-tuple-element.21), channel_id=1, source_target_pairs={{0,2},{1,3},{2,4},{3,5},{4,6},{5,7},{6,0},{7,1},{8,10},{9,11},{10,... | collective-permute-start | bytes 835592 | tf_op jit(solution)/shard_map/ppermute | solution.py:719
  62.3 1.2 %collective-permute-start.11 = (bf16[64,2176]{1,0:T(8,128)(2,1)S(1)}, bf16[64,2176]{1,0:T(8,128)(2,1)S(1)}, u32[]{:S(2)}, u32[]{:S(2)}) collective-permute-start(bf16[64,2176]{1,0:T(8,128)(2,1)S(1)} %get-tuple-element.22), channel_id=1, source_target_pairs={{0,4},{1,5},{2,6},{3,7},{4,0},{5,1},{6,2},{7,3},{8,12},{9,13},{10,... | collective-permute-start | bytes 835592 | tf_op jit(solution)/shard_map/ppermute | solution.py:719
  63.5 1.3 %collective-permute-start.12 = (bf16[64,2176]{1,0:T(8,128)(2,1)S(1)}, bf16[64,2176]{1,0:T(8,128)(2,1)S(1)}, u32[]{:S(2)}, u32[]{:S(2)}) collective-permute-start(bf16[64,2176]{1,0:T(8,128)(2,1)S(1)} %get-tuple-element.23), channel_id=1, source_target_pairs={{0,6},{1,7},{2,0},{3,1},{4,2},{5,3},{6,4},{7,5},{8,14},{9,15},{10,... | collective-permute-start | bytes 835592 | tf_op jit(solution)/shard_map/ppermute | solution.py:719
  64.8 5.1 %collective-permute-done.13.far = bf16[1280,128]{1,0:T(8,128)(2,1)S(1)} collective-permute-done((bf16[1280,128]{1,0:T(8,128)(2,1)S(1)}, bf16[1280,128]{1,0:T(8,128)(2,1)S(1)}, u32[]{:S(2)}, u32[]{:S(2)}) %collective-permute-start.13) | collective-permute-done | bytes 327712 | tf_op jit(solution)/shard_map/ppermute | solution.py:716
  69.9 0.6 choose.1.own
  70.5 0.9 %collective-permute-start.14 = (bf16[1280,128]{1,0:T(8,128)(2,1)S(1)}, bf16[1280,128]{1,0:T(8,128)(2,1)S(1)}, u32[]{:S(2)}, u32[]{:S(2)}) collective-permute-start(bf16[1280,128]{1,0:T(8,128)(2,1)S(1)} %choose.1.own), channel_id=1, source_target_pairs={{0,1},{1,0},{2,3},{3,2},{4,5},{5,4},{6,7},{7,6},{8,9},{9,8},{10,11... | collective-permute-start | bytes 983048 | tf_op jit(solution)/shard_map/ppermute | solution.py:722
  71.4 4.6 %collective-permute-done.11.b = bf16[64,2176]{1,0:T(8,128)(2,1)S(1)} collective-permute-done((bf16[64,2176]{1,0:T(8,128)(2,1)S(1)}, bf16[64,2176]{1,0:T(8,128)(2,1)S(1)}, u32[]{:S(2)}, u32[]{:S(2)}) %collective-permute-start.11) | collective-permute-done | bytes 278560 | tf_op jit(solution)/shard_map/ppermute | solution.py:719
  76.3 0.8 %sum_parts.1 = (bf16[64,2048]{1,0:T(8,128)(2,1)}, f32[4,2048]{1,0:T(4,128)S(1)}) custom-call(f32[64,2176]{1,0:T(8,128)S(1)} %get-tuple-element.20.own, bf16[64,2176]{1,0:T(8,128)(2,1)S(1)} %collective-permute-done.10.a, bf16[64,2176]{1,0:T(8,128)(2,1)S(1)} %collective-permute-done.11.b, bf16[64,2176]{1,0:T(8,128)(2,1)S(1)} %collective-permute-done.12.c), custom_call_target="tpu_custom_call" | custom-call | flops 40000000000 | bytes 2097152 | tf_op jit(solution)/shard_map/sum_parts/pallas_call | solution.py:590
  77.1 1.5 %collective-permute-start.15 = (f32[4,2048]{1,0:T(4,128)S(1)}, f32[4,2048]{1,0:T(4,128)S(1)}, u32[]{:S(2)}, u32[]{:S(2)}) collective-permute-start(f32[4,2048]{1,0:T(4,128)S(1)} %get-tuple-element.26), channel_id=1, source_target_pairs={{0,1},{1,0},{2,3},{3,2},{4,5},{5,4},{6,7},{7,6},{8,9},{9,8},{10,11... | collective-permute-start | bytes 98312 | tf_op jit(solution)/shard_map/ppermute | solution.py:722
  78.6 1.1 %cache.1 = bf16[576,512]{1,0:T(8,128)(2,1)} custom-call(bf16[1280,128]{1,0:T(8,128)(2,1)S(1)} %choose.1.own, bf16[1280,128]{1,0:T(8,128)(2,1)S(1)} %collective-permute-done.14.came), custom_call_target="tpu_custom_call" | custom-call | tf_op jit(solution)/shard_map/cache/pallas_call | solution.py:695
  79.7 0.6 add_convert_fusion
  (41 shorter events, 1.6 us)
Async XLA Ops:
  0.6 7.4 %copy-start = (bf16[2048,576]{0,1:T(8,128)(2,1)S(1)}, bf16[2048,576]{0,1:T(8,128)(2,1)}, u32[]{:S(2)}) copy-start(bf16[2048,576]{0,1:T(8,128)(2,1)} %param.15) | copy-start | bytes 7077892
  0.6 7.4 %copy-start.1 = (bf16[2048,384]{1,0:T(8,128)(2,1)S(1)}, bf16[2048,384]{1,0:T(8,128)(2,1)}, u32[]{:S(2)}) copy-start(bf16[2048,384]{1,0:T(8,128)(2,1)} %w.1) | copy-start | bytes 4718596
  0.7 7.4 %copy-start.7 = (f32[32,1]{1,0:T(8,128)S(1)}, f32[32,1]{1,0:T(8,128)}, u32[]{:S(2)}) copy-start(f32[32,1]{1,0:T(8,128)} %constant.2.clone.freq) | copy-start | bytes 388
  0.7 7.4 %copy-start.8 = (bf16[4,2048]{1,0:T(4,128)(2,1)S(1)}, bf16[4,2048]{1,0:T(4,128)(2,1)}, u32[]{:S(2)}) copy-start(bf16[4,2048]{1,0:T(4,128)(2,1)} %x.4) | copy-start | bytes 49156
  0.7 7.4 %copy-start.9 = (f32[512]{0:T(512)S(1)}, f32[512]{0:T(512)}, u32[]{:S(2)}) copy-start(f32[512]{0:T(512)} %param.16) | copy-start | bytes 6148
  0.7 7.4 %copy-start.10 = (s32[4]{0:T(128)S(1)}, s32[4]{0:T(128)}, u32[]{:S(2)}) copy-start(s32[4]{0:T(128)} %lengths.9) | copy-start | bytes 52
  4.9 3.1 %collective-permute-start = (bf16[1152,128]{1,0:T(8,128)(2,1)}, bf16[1152,128]{1,0:T(8,128)(2,1)S(1)}, u32[]{:S(2)}, u32[]{:S(2)}) collective-permute-start(bf16[1152,128]{1,0:T(8,128)(2,1)} %latent.1.half.refs_0_.own), channel_id=1, source_target_pairs={{0,1},{1,0},{2,3},{3,2},{4,5},{5,4},{6,7},{7,6},{8,9},{9,8},{10,11... | collective-permute-start | bytes 884744 | tf_op jit(solution)/shard_map/ppermute | solution.py:722
  6.3 14.0 %collective-permute-start.3 = (bf16[1152,128]{1,0:T(8,128)(2,1)}, bf16[1152,128]{1,0:T(8,128)(2,1)}, u32[]{:S(2)}, u32[]{:S(2)}) collective-permute-start(bf16[1152,128]{1,0:T(8,128)(2,1)} %latent.1.half.refs_0_.own), channel_id=1, source_target_pairs={{0,8},{1,9},{2,26},{3,27},{4,20},{5,21},{6,38},{7,39},{8,16},{9,17... | collective-permute-start | bytes 884744 | tf_op jit(solution)/shard_map/ppermute | solution.py:716
  8.1 1.0 %copy-start.2 = (bf16[1152,128]{1,0:T(8,128)(2,1)S(1)}, bf16[1152,128]{1,0:T(8,128)(2,1)}, u32[]{:S(2)}) copy-start(bf16[1152,128]{1,0:T(8,128)(2,1)} %latent.1.half.refs_0_.own) | copy-start | bytes 884740
  9.1 1.0 %copy-start.5 = (bf16[512,512]{1,0:T(8,128)(2,1)S(1)}, bf16[512,512]{1,0:T(8,128)(2,1)}, u32[]{:S(2)}) copy-start(bf16[512,512]{1,0:T(8,128)(2,1)} %w_own.4) | copy-start | bytes 1572868
  13.5 18.1 %copy-start.6 = (bf16[512,512]{1,0:T(8,128)(2,1)S(1)}, bf16[512,512]{1,0:T(8,128)(2,1)}, u32[]{:S(2)}) copy-start(bf16[512,512]{1,0:T(8,128)(2,1)} %w_own.4) | copy-start | bytes 1572868
  20.3 9.6 %collective-permute-start.4 = (bf16[1152,128]{1,0:T(8,128)(2,1)}, bf16[1152,128]{1,0:T(8,128)(2,1)S(1)}, u32[]{:S(2)}, u32[]{:S(2)}) collective-permute-start(bf16[1152,128]{1,0:T(8,128)(2,1)} %passed.1.x.refs_1_.refs_0_), channel_id=1, source_target_pairs={{0,32},{1,33},{2,34},{3,35},{4,36},{5,37},{6,38},{7,39},{8,40},{9,... | collective-permute-start | bytes 884744 | tf_op jit(solution)/shard_map/ppermute | solution.py:716
  20.3 14.1 %all-to-all-start = ((f32[16,8,256]{2,1,0:T(8,128)}), f32[16,8,256]{2,1,0:T(8,128)S(1)}, u32[]{:S(2)}, u32[]{:S(2)}) async-start(f32[16,8,256]{2,1,0:T(8,128)} %bitcast.2), calls=%async_computation | async-start | bytes 262144 | tf_op jit(solution)/shard_map/all_to_all | solution.py:738
  30.0 15.5 %collective-permute-start.5 = (bf16[2304,128]{1,0:T(8,128)(2,1)S(1)}, bf16[2304,128]{1,0:T(8,128)(2,1)S(1)}, u32[]{:S(2)}, u32[]{:S(2)}) collective-permute-start(bf16[2304,128]{1,0:T(8,128)(2,1)S(1)} %second_part.1), channel_id=1, source_target_pairs={{0,6},{1,7},{2,0},{3,1},{4,2},{5,3},{6,4},{7,5},{8,14},{9,15},{10,... | collective-permute-start | bytes 1769480 | tf_op jit(solution)/shard_map/ppermute | solution.py:719
  30.1 16.0 %collective-permute-start.6 = (bf16[2304,128]{1,0:T(8,128)(2,1)S(1)}, bf16[2304,128]{1,0:T(8,128)(2,1)S(1)}, u32[]{:S(2)}, u32[]{:S(2)}) collective-permute-start(bf16[2304,128]{1,0:T(8,128)(2,1)S(1)} %second_part.1), channel_id=1, source_target_pairs={{0,8},{1,9},{2,10},{3,11},{4,124},{5,125},{6,126},{7,127},{8,16},{... | collective-permute-start | bytes 1769480 | tf_op jit(solution)/shard_map/ppermute | solution.py:716
  30.2 15.9 %collective-permute-start.7 = (bf16[2304,128]{1,0:T(8,128)(2,1)S(1)}, bf16[2304,128]{1,0:T(8,128)(2,1)S(1)}, u32[]{:S(2)}, u32[]{:S(2)}) collective-permute-start(bf16[2304,128]{1,0:T(8,128)(2,1)S(1)} %second_part.1), channel_id=1, source_target_pairs={{0,2},{1,3},{2,4},{3,5},{4,6},{5,7},{6,0},{7,1},{8,10},{9,11},{10,... | collective-permute-start | bytes 1769480 | tf_op jit(solution)/shard_map/ppermute | solution.py:719
  31.6 7.6 %collective-permute-start.2 = (bf16[512,512]{1,0:T(8,128)(2,1)S(1)}, bf16[512,512]{1,0:T(8,128)(2,1)}, u32[]{:S(2)}, u32[]{:S(2)}) collective-permute-start(bf16[512,512]{1,0:T(8,128)(2,1)S(1)} %copy-done.6), channel_id=1, source_target_pairs={{0,1},{1,0},{2,3},{3,2},{4,5},{5,4},{6,7},{7,6},{8,9},{9,8},{10,11... | collective-permute-start | bytes 1572872 | tf_op jit(solution)/shard_map/ppermute | solution.py:722
  34.4 4.4 %copy-start.4 = (bf16[256,2048]{1,0:T(8,128)(2,1)S(1)}, bf16[256,2048]{1,0:T(8,128)(2,1)}, u32[]{:S(2)}) copy-start(bf16[256,2048]{1,0:T(8,128)(2,1)} %w_own.5) | copy-start | bytes 3145732
  34.4 6.3 %copy-start.3 = (bf16[1152,128]{1,0:T(8,128)(2,1)S(1)}, bf16[1152,128]{1,0:T(8,128)(2,1)}, u32[]{:S(2)}) copy-start(bf16[1152,128]{1,0:T(8,128)(2,1)} %latent.1.half.refs_0_.own) | copy-start | bytes 884740
  38.7 2.0 %collective-permute-start.1 = (bf16[2,512,256]{2,1,0:T(8,128)(2,1)S(1)}, bf16[2,512,256]{2,1,0:T(8,128)(2,1)S(1)}, u32[]{:S(2)}, u32[]{:S(2)}) collective-permute-start(bf16[2,512,256]{2,1,0:T(8,128)(2,1)S(1)} %query.1.q_own), channel_id=1, source_target_pairs={{0,1},{1,0},{2,3},{3,2},{4,5},{5,4},{6,7},{7,6},{8,9},{9,8},{10,11... | collective-permute-start | bytes 1572872 | tf_op jit(solution)/shard_map/ppermute | solution.py:722
  39.2 20.0 %collective-permute-start.9 = (bf16[256,2048]{1,0:T(8,128)(2,1)S(1)}, bf16[256,2048]{1,0:T(8,128)(2,1)S(1)}, u32[]{:S(2)}, u32[]{:S(2)}) collective-permute-start(bf16[256,2048]{1,0:T(8,128)(2,1)S(1)} %copy-done.4), channel_id=1, source_target_pairs={{0,1},{1,0},{2,3},{3,2},{4,5},{5,4},{6,7},{7,6},{8,9},{9,8},{10,11... | collective-permute-start | bytes 3145736 | tf_op jit(solution)/shard_map/ppermute | solution.py:722
  45.5 12.1 %copy-start.11 = (s32[64]{0:T(128)S(1)}, s32[64]{0:T(128)}, u32[]{:S(2)}) copy-start(s32[64]{0:T(128)} %table.3) | copy-start | bytes 772
  54.3 5.0 %collective-permute-start.8 = (f32[256,640]{1,0:T(8,128)S(1)}, f32[256,640]{1,0:T(8,128)S(1)}, u32[]{:S(2)}, u32[]{:S(2)}) collective-permute-start(f32[256,640]{1,0:T(8,128)S(1)} %get-tuple-element.18), channel_id=1, source_target_pairs={{0,1},{1,0},{2,3},{3,2},{4,5},{5,4},{6,7},{7,6},{8,9},{9,8},{10,11... | collective-permute-start | bytes 1966088 | tf_op jit(solution)/shard_map/ppermute | solution.py:722
  58.8 11.1 %collective-permute-start.13 = (bf16[1280,128]{1,0:T(8,128)(2,1)S(1)}, bf16[1280,128]{1,0:T(8,128)(2,1)S(1)}, u32[]{:S(2)}, u32[]{:S(2)}) collective-permute-start(bf16[1280,128]{1,0:T(8,128)(2,1)S(1)} %get-tuple-element.25), channel_id=1, source_target_pairs={{0,64},{1,65},{2,66},{3,67},{4,68},{5,69},{6,70},{7,71},{8,72},{9,... | collective-permute-start | bytes 983048 | tf_op jit(solution)/shard_map/ppermute | solution.py:716
  60.9 10.5 %collective-permute-start.10 = (bf16[64,2176]{1,0:T(8,128)(2,1)S(1)}, bf16[64,2176]{1,0:T(8,128)(2,1)S(1)}, u32[]{:S(2)}, u32[]{:S(2)}) collective-permute-start(bf16[64,2176]{1,0:T(8,128)(2,1)S(1)} %get-tuple-element.21), channel_id=1, source_target_pairs={{0,2},{1,3},{2,4},{3,5},{4,6},{5,7},{6,0},{7,1},{8,10},{9,11},{10,... | collective-permute-start | bytes 835592 | tf_op jit(solution)/shard_map/ppermute | solution.py:719
  62.3 13.7 %collective-permute-start.11 = (bf16[64,2176]{1,0:T(8,128)(2,1)S(1)}, bf16[64,2176]{1,0:T(8,128)(2,1)S(1)}, u32[]{:S(2)}, u32[]{:S(2)}) collective-permute-start(bf16[64,2176]{1,0:T(8,128)(2,1)S(1)} %get-tuple-element.22), channel_id=1, source_target_pairs={{0,4},{1,5},{2,6},{3,7},{4,0},{5,1},{6,2},{7,3},{8,12},{9,13},{10,... | collective-permute-start | bytes 835592 | tf_op jit(solution)/shard_map/ppermute | solution.py:719
  63.5 12.8 %collective-permute-start.12 = (bf16[64,2176]{1,0:T(8,128)(2,1)S(1)}, bf16[64,2176]{1,0:T(8,128)(2,1)S(1)}, u32[]{:S(2)}, u32[]{:S(2)}) collective-permute-start(bf16[64,2176]{1,0:T(8,128)(2,1)S(1)} %get-tuple-element.23), channel_id=1, source_target_pairs={{0,6},{1,7},{2,0},{3,1},{4,2},{5,3},{6,4},{7,5},{8,14},{9,15},{10,... | collective-permute-start | bytes 835592 | tf_op jit(solution)/shard_map/ppermute | solution.py:719
  70.5 8.1 %collective-permute-start.14 = (bf16[1280,128]{1,0:T(8,128)(2,1)S(1)}, bf16[1280,128]{1,0:T(8,128)(2,1)S(1)}, u32[]{:S(2)}, u32[]{:S(2)}) collective-permute-start(bf16[1280,128]{1,0:T(8,128)(2,1)S(1)} %choose.1.own), channel_id=1, source_target_pairs={{0,1},{1,0},{2,3},{3,2},{4,5},{5,4},{6,7},{7,6},{8,9},{9,8},{10,11... | collective-permute-start | bytes 983048 | tf_op jit(solution)/shard_map/ppermute | solution.py:722
  77.1 2.6 %collective-permute-start.15 = (f32[4,2048]{1,0:T(4,128)S(1)}, f32[4,2048]{1,0:T(4,128)S(1)}, u32[]{:S(2)}, u32[]{:S(2)}) collective-permute-start(f32[4,2048]{1,0:T(4,128)S(1)} %get-tuple-element.26), channel_id=1, source_target_pairs={{0,1},{1,0},{2,3},{3,2},{4,5},{5,4},{6,7},{7,6},{8,9},{9,8},{10,11... | collective-permute-start | bytes 98312 | tf_op jit(solution)/shard_map/ppermute | solution.py:722
